TPU v7x, 768 devices: a whole 4x8x12 slice. The times are simulated.
768 devices in a mesh: gx: 48 (over x, z), gy: 16 (over y, core).
Axes of the slice: x: 4, y: 8, z: 12, core: 2. Of those that a mesh axis runs over, the one named last changes fastest.
Arguments:
- displacement: float32 [384, 64, 3, 128], P('gx', 'gy'), may hold values from -6 to 6
- volume: float32 [384, 64, 128], P('gx', 'gy'), may hold values from 0.5 to 2
- health: float32 [384, 64, 128], P('gx', 'gy'), may hold values from 0.2 to 1
- damage: int32 [384, 64, 128], P('gx', 'gy'), may hold values 0 or 1
- block_pairs: int32 [48, 16, 162, 4], P('gx', 'gy'), may hold values from -1 to 9, as said below
Outputs:
- deform_grad: float32 [384, 64, 9, 128], P('gx', 'gy')
- force_density: float32 [384, 64, 3, 128], P('gx', 'gy')
Inputs may be any that keep to these rules, and one draw needn't show every extreme that they name: `block_pairs`: every row is (ax, ay, bx, by) with blocks in a device's frame: its own blocks at 1 to 8 and 1 to 4, the blocks beside them at 0 and 9, 0 and 5; (bx - ax, by - ay) is (1, 0), (0, 1), (1, 1) or (1, -1); both blocks lie inside the plate and at least one is the device's own. A pair of adjacent plate blocks is named at most once over all devices; pairs named nowhere are severed. Live rows come first, then rows of -1. In every draw some device names all 162 pairs that touch its blocks.
All inputs are finite; a program needn't handle non-finite values. No bound on the sum of `damage` on one device may be relied on, other than what follows from the above.
Results may differ from a plain program's by a relative error of at most 0.0003.
Values sent between devices are 32-bit elements; how exact they have to be, the bound alone decides.
A program may use at most 32 MiB of HBM per device.

v0:
```python
import jax
import jax.numpy as jnp
import numpy as np
from jax import lax
from jax.sharding import PartitionSpec as P

highest = lax.Precision.HIGHEST
lame_first = 24.0
shear_modulus = 16.0
transpose_order = np.array([0, 3, 6, 1, 4, 7, 2, 5, 8])


def from_behind(array, axis, by):
    size = lax.axis_size(axis)
    pairs = [(i, i + by) for i in range(size) if 0 <= i + by < size]
    return lax.ppermute(array, axis, pairs)


def with_halo(block, sides, width):
    for axis, dim in sides:
        count = lax.axis_size(axis)
        forward = [(i, i + 1) for i in range(count - 1)]
        backward = [(target, source) for source, target in forward]
        low = lax.ppermute(
            lax.slice_in_dim(block, block.shape[dim] - width, None, axis=dim), axis, forward
        )
        high = lax.ppermute(lax.slice_in_dim(block, 0, width, axis=dim), axis, backward)
        block = jnp.concatenate([low, block, high], axis=dim)
    return block


def lattice(points):
    index = jnp.arange(points, dtype=jnp.int32)
    return jnp.stack([index % 4, index // 4 % 4, index // 16])


def block_offset(step_x, step_y):
    return jnp.stack([4 * step_x, 4 * step_y, jnp.zeros_like(step_x)], axis=1)


def bond_weights(health_first, health_second, step_x, step_y):
    points = health_first.shape[-1]
    lattice_grid = lattice(points)
    shifted = lattice_grid[None] + block_offset(step_x, step_y)[:, :, None]
    distance = jnp.zeros((step_x.shape[0], points, points), jnp.int32)
    for comp_index in range(3):
        gap_comp = shifted[:, comp_index, None, :] - lattice_grid[None, comp_index, :, None]
        distance = distance + gap_comp * gap_comp
    linked = (distance <= 9) & (distance > 0)
    lower_health = jnp.minimum(health_first[:, :, None], health_second[:, None, :])
    return jnp.where(linked, lower_health, jnp.zeros_like(lower_health))


def positions(point_pack, step_x, step_y):
    reference_pos = (
        lattice(point_pack.shape[-1])[None] + block_offset(step_x, step_y)[:, :, None]
    ).astype(jnp.float32)
    return (reference_pos, reference_pos + point_pack[:, 0:3], point_pack[:, 3], point_pack[:, 4])


def shape_features(ref_pos, cur_pos, vol_pts):
    slot_count, points = (ref_pos.shape[0], ref_pos.shape[-1])
    outer_rr = (ref_pos[:, :, None] * ref_pos[:, None]).reshape(slot_count, 9, points)
    outer_cr = (cur_pos[:, :, None] * ref_pos[:, None]).reshape(slot_count, 9, points)
    ones_row = jnp.ones((slot_count, 1, points), jnp.float32)
    return (
        jnp.concatenate([outer_rr, outer_cr, ref_pos, cur_pos, ones_row], axis=1) * vol_pts[:, None]
    )


def shape_terms(tile_sums, ref_pos, cur_pos):
    slot_count, points = (ref_pos.shape[0], ref_pos.shape[-1])
    sum_rr = tile_sums[:, 0:9].reshape(slot_count, 3, 3, points)
    sum_cr = tile_sums[:, 9:18].reshape(slot_count, 3, 3, points)
    sum_r = tile_sums[:, 18:21]
    sum_c = tile_sums[:, 21:24]
    sum_one = tile_sums[:, 24][:, None, None]
    shape_k = (
        sum_rr
        - ref_pos[:, :, None] * sum_r[:, None]
        - sum_r[:, :, None] * ref_pos[:, None]
        + sum_one * ref_pos[:, :, None] * ref_pos[:, None]
    )
    shape_n = (
        sum_cr
        - cur_pos[:, :, None] * sum_r[:, None]
        - sum_c[:, :, None] * ref_pos[:, None]
        + sum_one * cur_pos[:, :, None] * ref_pos[:, None]
    )
    return jnp.concatenate(
        [shape_k.reshape(slot_count, 9, points), shape_n.reshape(slot_count, 9, points)], axis=1
    )


def force_features(ref_pos, stress_map, vol_pts):
    slot_count, points = (ref_pos.shape[0], ref_pos.shape[-1])
    mapped = jnp.sum(stress_map * ref_pos[:, None], axis=2)
    ones_row = jnp.ones((slot_count, 1, points), jnp.float32)
    return (
        jnp.concatenate(
            [mapped, stress_map.reshape(slot_count, 9, points), ref_pos, ones_row], axis=1
        )
        * vol_pts[:, None]
    )


def force_terms(tile_sums, ref_pos, stress_map):
    slot_count, points = (ref_pos.shape[0], ref_pos.shape[-1])
    sum_ar = tile_sums[:, 0:3]
    sum_a = tile_sums[:, 3:12].reshape(slot_count, 3, 3, points)
    spread = tile_sums[:, 12:15] - tile_sums[:, 15][:, None] * ref_pos
    return (
        jnp.sum(stress_map * spread[:, None], axis=2)
        + sum_ar
        - jnp.sum(sum_a * ref_pos[:, None], axis=2)
    )


def tile_terms(pack_first, pack_second, map_first, map_second, step_x, step_y, section):
    zero_step = jnp.zeros_like(step_x)
    ref_a, cur_a, vol_a, health_a = positions(pack_first, zero_step, zero_step)
    ref_b, cur_b, vol_b, health_b = positions(pack_second, step_x, step_y)
    weights = bond_weights(health_a, health_b, step_x, step_y)
    if section == "shape":
        feat_a = shape_features(ref_a, cur_a, vol_a)
        feat_b = shape_features(ref_b, cur_b, vol_b)
    else:
        feat_a = force_features(ref_a, map_first, vol_a)
        feat_b = force_features(ref_b, map_second, vol_b)
    sums_a = jnp.einsum("gcj,gij->gci", feat_b, weights, precision=highest)
    sums_b = jnp.einsum("gci,gij->gcj", feat_a, weights, precision=highest)
    if section == "shape":
        return (shape_terms(sums_a, ref_a, cur_a), shape_terms(sums_b, ref_b, cur_b))
    return (force_terms(sums_a, ref_a, map_first), force_terms(sums_b, ref_b, map_second))


def block_sums(row_pack, row_map, section):
    rows_count, points = (row_pack.shape[0], row_pack.shape[-1])
    zero_step = jnp.zeros((rows_count,), jnp.int32)
    ref_pos, cur_pos, vol_pts, health_pts = positions(row_pack, zero_step, zero_step)
    weights = bond_weights(health_pts, health_pts, zero_step, zero_step)
    if section == "shape":
        feats = shape_features(ref_pos, cur_pos, vol_pts)
        return shape_terms(
            jnp.einsum("gcj,gij->gci", feats, weights, precision=highest), ref_pos, cur_pos
        )
    stress_map = row_map.reshape(rows_count, 3, 3, points)
    feats = force_features(ref_pos, stress_map, vol_pts)
    return force_terms(
        jnp.einsum("gcj,gij->gci", feats, weights, precision=highest), ref_pos, stress_map
    )


def pair_sums(ext_pack, ext_map, slot_list, section):
    ext_x, ext_y, fields, points = ext_pack.shape
    blocks = ext_x * ext_y
    flat_pack = ext_pack.reshape(blocks, fields, points)
    slot_count = slot_list.shape[0]
    turn_count = min(slot_count, 20)
    group_size = -(-slot_count // turn_count)
    filler = jnp.full((group_size * turn_count - slot_count, 4), -1, jnp.int32)
    padded_slots = jnp.concatenate([slot_list, filler], axis=0)
    comp_width = 18 if section == "shape" else 3
    block_ids = jnp.arange(blocks, dtype=jnp.int32)

    def one_group(running, group_slots):
        usable = group_slots[:, 0] >= 0
        first_block = jnp.where(usable, group_slots[:, 0] * ext_y + group_slots[:, 1], 0)
        second_block = jnp.where(usable, group_slots[:, 2] * ext_y + group_slots[:, 3], 0)
        step_x = jnp.where(usable, group_slots[:, 2] - group_slots[:, 0], 0)
        step_y = jnp.where(usable, group_slots[:, 3] - group_slots[:, 1], 0)
        if section == "shape":
            map_first, map_second = (None, None)
        else:
            flat_map = ext_map.reshape(blocks, 3, 3, points)
            map_first, map_second = (flat_map[first_block], flat_map[second_block])
        to_first, to_second = tile_terms(
            flat_pack[first_block],
            flat_pack[second_block],
            map_first,
            map_second,
            step_x,
            step_y,
            section,
        )
        hit_first = ((first_block[:, None] == block_ids[None]) & usable[:, None]).astype(
            jnp.float32
        )
        hit_second = ((second_block[:, None] == block_ids[None]) & usable[:, None]).astype(
            jnp.float32
        )
        running = running + jnp.dot(
            hit_first.T,
            to_first.reshape(group_size, comp_width * points),
            precision=highest,
            preferred_element_type=jnp.float32,
        )
        running = running + jnp.dot(
            hit_second.T,
            to_second.reshape(group_size, comp_width * points),
            precision=highest,
            preferred_element_type=jnp.float32,
        )
        return (running, None)

    running, _ = lax.scan(
        one_group,
        jnp.zeros((blocks, comp_width * points), jnp.float32),
        padded_slots.reshape(turn_count, group_size, 4),
    )
    return running.reshape(ext_x, ext_y, comp_width, points)


def product_three(left_mat, right_mat):
    entry_list = []
    for row_index in range(3):
        for col_index in range(3):
            entry_list.append(
                left_mat[..., 3 * row_index, :] * right_mat[..., col_index, :]
                + left_mat[..., 3 * row_index + 1, :] * right_mat[..., 3 + col_index, :]
                + left_mat[..., 3 * row_index + 2, :] * right_mat[..., 6 + col_index, :]
            )
    return jnp.stack(entry_list, axis=-2)


def invert_three(matrix):
    entry = [matrix[..., slot_index, :] for slot_index in range(9)]
    cof_00 = entry[4] * entry[8] - entry[5] * entry[7]
    cof_01 = entry[5] * entry[6] - entry[3] * entry[8]
    cof_02 = entry[3] * entry[7] - entry[4] * entry[6]
    cof_10 = entry[2] * entry[7] - entry[1] * entry[8]
    cof_11 = entry[0] * entry[8] - entry[2] * entry[6]
    cof_12 = entry[1] * entry[6] - entry[0] * entry[7]
    cof_20 = entry[1] * entry[5] - entry[2] * entry[4]
    cof_21 = entry[2] * entry[3] - entry[0] * entry[5]
    cof_22 = entry[0] * entry[4] - entry[1] * entry[3]
    determinant = entry[0] * cof_00 + entry[1] * cof_01 + entry[2] * cof_02
    adjugate = jnp.stack(
        [cof_00, cof_10, cof_20, cof_01, cof_11, cof_21, cof_02, cof_12, cof_22], axis=-2
    )
    return adjugate / determinant[..., None, :]


def material(shape_sums, damage):
    identity = jnp.eye(3, dtype=jnp.float32).reshape(9)[:, None]
    inverse = invert_three(shape_sums[..., 0:9, :] + identity)
    deform_grad = product_three(shape_sums[..., 9:18, :], inverse)
    strain = 0.5 * (product_three(deform_grad[..., transpose_order, :], deform_grad) - identity)
    strain_trace = strain[..., 0, :] + strain[..., 4, :] + strain[..., 8, :]
    second_pk = lame_first * strain_trace[..., None, :] * identity + 2.0 * shear_modulus * strain
    first_pk = (
        product_three(deform_grad, second_pk) * (1.0 - damage.astype(jnp.float32))[..., None, :]
    )
    return (deform_grad, product_three(first_pk, inverse))


def pass_x(rim_piece, step):
    return from_behind(rim_piece, "gx", step)


def pass_y(rim_piece, step):
    return from_behind(rim_piece, "gy", step)


def give_back(ext_sums):
    inner_x = ext_sums.shape[0] - 2
    inner_y = ext_sums.shape[1] - 2
    own_sums = ext_sums[1 : inner_x + 1, 1 : inner_y + 1]
    own_sums = own_sums.at[:, inner_y - 1].add(pass_y(ext_sums[1 : inner_x + 1, 0], -1))
    own_sums = own_sums.at[:, 0].add(pass_y(ext_sums[1 : inner_x + 1, inner_y + 1], 1))
    own_sums = own_sums.at[inner_x - 1].add(pass_x(ext_sums[0, 1 : inner_y + 1], -1))
    own_sums = own_sums.at[0].add(pass_x(ext_sums[inner_x + 1, 1 : inner_y + 1], 1))
    own_sums = own_sums.at[inner_x - 1, inner_y - 1].add(pass_y(pass_x(ext_sums[0, 0], -1), -1))
    own_sums = own_sums.at[0, inner_y - 1].add(pass_y(pass_x(ext_sums[inner_x + 1, 0], 1), -1))
    own_sums = own_sums.at[inner_x - 1, 0].add(pass_y(pass_x(ext_sums[0, inner_y + 1], -1), 1))
    own_sums = own_sums.at[0, 0].add(pass_y(pass_x(ext_sums[inner_x + 1, inner_y + 1], 1), 1))
    return own_sums


def local(displacement, volume, health, damage, block_pairs):
    point_pack = jnp.concatenate([displacement, volume[:, :, None], health[:, :, None]], axis=2)
    ext_pack = with_halo(point_pack, (("gx", 0), ("gy", 1)), 1)
    own_shape = lax.map(lambda row_pack: block_sums(row_pack, None, "shape"), point_pack)
    slot_list = block_pairs[0, 0]
    shape_sums = give_back(pair_sums(ext_pack, None, slot_list, "shape")) + own_shape
    deform_grad, stress_map = material(shape_sums, damage)
    ext_map = with_halo(stress_map, (("gx", 0), ("gy", 1)), 1)
    own_force = lax.map(
        lambda row_items: block_sums(row_items[0], row_items[1], "force"), (point_pack, stress_map)
    )
    force_density = give_back(pair_sums(ext_pack, ext_map, slot_list, "force")) + own_force
    return (deform_grad, force_density)


def solution(mesh):
    in_specs = (
        P("gx", "gy", None, None),
        P("gx", "gy", None),
        P("gx", "gy", None),
        P("gx", "gy", None),
        P("gx", "gy", None, None),
    )
    out_specs = (P("gx", "gy", None, None), P("gx", "gy", None, None))
    return jax.shard_map(local, mesh=mesh, in_specs=in_specs, out_specs=out_specs, check_vma=False)
```

profile of v0, /device:TPU:31, one launch (start us, length us, event | category | flops | bytes accessed | tf_op | source)
XLA Modules:
  0.0 409.8 jit_solution(928590623317155731)
XLA Ops:
  1.5 4.0 collective-permute-start
  5.5 12.5 %collective-permute-start.1 = (f32[1,4,5,128]{3,1,2,0:T(4,128)S(1)}, f32[1,4,5,128]{3,1,2,0:T(4,128)S(1)}, u32[]{:S(2)}, u32[]{:S(2)}) collective-permute-start(f32[1,4,5,128]{3,1,2,0:T(4,128)S(1)} %get-tuple-element.892), channel_id=1, source_target_pairs={{16,0},{32,16},{48,32},{64,48},{80,64},{96,80},{112,96},{128,112},... | collective-permute-start | bytes 30728 | tf_op jit(solution)/shard_map/ppermute | solution.py:27
  18.6 12.1 %while.73 = (s32[]{:T(128)}, f32[8,4,18,128]{3,0,2,1:T(8,128)S(1)}, f32[8,4,5,128]{3,1,2,0:T(4,128)S(1)}, s32[]{:T(128)}, f32[]{:T(128)}, /*index=5*/s32[]{:T(128)}) while((s32[]{:T(128)}, f32[8,4,18,128]{3,0,2,1:T(8,128)S(1)}, f32[8,4,5,128]{3,1,2,0:T(4,128)S(1)}, s32[]{:T(128)}, f32[]{:T(128)}, /*index=5*/s32[]{:T(128)}) %tuple.385), condition=%wide.region_4.5_spmd, body=%wide.region_3.4_spmd.sunk | while | flops 20611072 | bytes 1072721 | solution.py:283
  31.6 5.3 %collective-permute-start.2 = (f32[10,1,5,128]{3,1,2,0:T(1,128)S(1)}, f32[10,1,5,128]{3,1,2,0:T(1,128)S(1)}, u32[]{:S(2)}, u32[]{:S(2)}) collective-permute-start(f32[10,1,5,128]{3,1,2,0:T(1,128)S(1)} %get-tuple-element.889), channel_id=1, source_target_pairs={{0,1},{1,2},{2,3},{3,4},{4,5},{5,6},{6,7},{7,8},{8,9},{9,10},{10,1... | collective-permute-start | bytes 76808 | tf_op jit(solution)/shard_map/ppermute | solution.py:24
  36.9 1.9 collective-permute-start.3
  39.0 4.2 %collective-permute-done.3 = f32[10,1,5,128]{3,1,2,0:T(1,128)S(1)} collective-permute-done((f32[10,1,5,128]{3,1,2,0:T(1,128)S(1)}, f32[10,1,5,128]{3,1,2,0:T(1,128)S(1)}, u32[]{:S(2)}, u32[]{:S(2)}) %collective-permute-start.3) | collective-permute-done | bytes 25632 | tf_op jit(solution)/shard_map/ppermute | solution.py:27
  43.4 129.9 %while.75 = (s32[]{:T(128)}, f32[60,2304]{1,0:T(8,128)S(1)}, s32[20,9,4]{1,2,0:T(4,128)S(1)}, f32[60,5,128]{2,1,0:T(8,128)S(1)}, s32[]{:T(128)}, /*index=5*/f32[]{:T(128)}, s32[]{:T(128)}, f32[]{:T(128)}) while((s32[]{:T(128)}, f32[60,2304]{1,0:T(8,128)S(1)}, s32[20,9,4]{1,2,0:T(4,128)S(1)}, ...), condition=%wide.region_1.2_spmd.clone.clone, body=%wide.region_0.1_spmd.clone.clone.sunk | while | flops 123013720 | bytes 8238270 | solution.py:206
  47.0 1.3 fusion.261
  53.5 1.3 fusion.261
  60.0 1.3 fusion.261
  66.5 1.3 fusion.261
  73.0 1.3 fusion.261
  92.5 1.3 fusion.261
  125.0 1.3 fusion.261
  137.9 1.3 fusion.261
  170.4 1.3 fusion.261
  173.4 1.9 collective-permute-start.4
  175.3 4.9 %collective-permute-start.5 = (f32[8,18,128]{2,1,0:T(8,128)S(1)}, f32[8,18,128]{2,1,0:T(8,128)S(1)}, u32[]{:S(2)}, u32[]{:S(2)}) collective-permute-start(f32[8,18,128]{2,1,0:T(8,128)S(1)} %get-tuple-element.875), channel_id=1, source_target_pairs={{0,1},{1,2},{2,3},{3,4},{4,5},{5,6},{6,7},{7,8},{8,9},{9,10},{10,1... | collective-permute-start | bytes 221192 | tf_op jit(solution)/shard_map/ppermute | solution.py:16
  180.2 3.6 collective-permute-start.6
  183.9 2.2 collective-permute-start.8
  186.0 3.1 collective-permute-start.10
  189.2 4.3 %collective-permute-start.12 = (f32[18,128]{1,0:T(8,128)S(1)}, f32[18,128]{1,0:T(8,128)S(1)}, u32[]{:S(2)}, u32[]{:S(2)}) collective-permute-start(f32[18,128]{1,0:T(8,128)S(1)} %get-tuple-element.870), channel_id=1, source_target_pairs={{16,0},{32,16},{48,32},{64,48},{80,64},{96,80},{112,96},{128,112},... | collective-permute-start | bytes 27656 | tf_op jit(solution)/shard_map/ppermute | solution.py:16
  193.5 1.9 collective-permute-start.14
  195.5 1.9 collective-permute-start.7
  197.4 1.9 collective-permute-start.9
  199.3 1.9 collective-permute-start.11
  201.3 4.9 %collective-permute-start.13 = (f32[18,128]{1,0:T(8,128)S(1)}, f32[18,128]{1,0:T(8,128)S(1)}, u32[]{:S(2)}, u32[]{:S(2)}) collective-permute-start(f32[18,128]{1,0:T(8,128)S(1)} %collective-permute-done.12), channel_id=1, source_target_pairs={{0,1},{1,2},{2,3},{3,4},{4,5},{5,6},{6,7},{7,8},{8,9},{9,10},{10,1... | collective-permute-start | bytes 27656 | tf_op jit(solution)/shard_map/ppermute | solution.py:16
  206.2 2.4 collective-permute-start.15
  208.7 1.7 fusion.160
  212.5 1.9 collective-permute-start.16
  214.4 5.5 %collective-permute-start.17 = (f32[1,4,9,128]{3,0,2,1:T(1,128)S(1)}, f32[1,4,9,128]{3,0,2,1:T(1,128)S(1)}, u32[]{:S(2)}, u32[]{:S(2)}) collective-permute-start(f32[1,4,9,128]{3,0,2,1:T(1,128)S(1)} %get-tuple-element.880), channel_id=1, source_target_pairs={{16,0},{32,16},{48,32},{64,48},{80,64},{96,80},{112,96},{128,112},... | collective-permute-start | bytes 55304 | tf_op jit(solution)/shard_map/ppermute | solution.py:27
  220.8 5.3 %collective-permute-start.18 = (f32[10,1,9,128]{3,0,2,1:T(8,128)S(1)}, f32[10,1,9,128]{3,0,2,1:T(8,128)S(1)}, u32[]{:S(2)}, u32[]{:S(2)}) collective-permute-start(f32[10,1,9,128]{3,0,2,1:T(8,128)S(1)} %get-tuple-element.877), channel_id=1, source_target_pairs={{0,1},{1,2},{2,3},{3,4},{4,5},{5,6},{6,7},{7,8},{8,9},{9,10},{10,1... | collective-permute-start | bytes 138248 | tf_op jit(solution)/shard_map/ppermute | solution.py:24
  226.1 2.1 collective-permute-start.19
  228.2 9.0 %while.74 = (s32[]{:T(128)}, f32[8,4,3,128]{3,2,1,0:T(4,128)S(1)}, f32[8,4,9,128]{3,0,2,1:T(8,128)S(1)}, f32[8,4,5,128]{3,1,2,0:T(4,128)S(1)}, s32[]{:T(128)}, /*index=5*/f32[]{:T(128)}, f32[]{:T(128)}) while((s32[]{:T(128)}, f32[8,4,3,128]{3,2,1,0:T(4,128)S(1)}, f32[8,4,9,128]{3,0,2,1:T(8,128)S(1)}, f32[8,4,5,128]{3,1,2,0:T(4,128)S(1)}, ...), condition=%wide.region_17.18_spmd, body=%wide.region_13.17_spmd.sunk | while | flops 13505922 | bytes 468705 | solution.py:288
  238.8 131.1 %while.76 = (s32[]{:T(128)}, f32[60,384]{1,0:T(8,128)S(1)}, s32[20,9,4]{1,2,0:T(4,128)S(1)}, f32[10,6,9,128]{3,1,0,2:T(8,128)}, f32[60,5,128]{2,1,0:T(8,128)S(1)...) while((s32[]{:T(128)}, f32[60,384]{1,0:T(8,128)S(1)}, ...), condition=%wide.wide.region_12.13_spmd.clone.clone, body=%wide.wide.region_5.12_spmd.clone.clone.sunk | while | flops 65808856 | bytes 2965474 | solution.py:206
  370.0 1.9 collective-permute-start.20
  372.0 4.9 %collective-permute-start.21 = (f32[8,3,128]{2,1,0:T(4,128)S(1)}, f32[8,3,128]{2,1,0:T(4,128)S(1)}, u32[]{:S(2)}, u32[]{:S(2)}) collective-permute-start(f32[8,3,128]{2,1,0:T(4,128)S(1)} %get-tuple-element.887), channel_id=1, source_target_pairs={{0,1},{1,2},{2,3},{3,4},{4,5},{5,6},{6,7},{7,8},{8,9},{9,10},{10,1... | collective-permute-start | bytes 36872 | tf_op jit(solution)/shard_map/ppermute | solution.py:16
  376.8 6.0 %collective-permute-start.22 = (f32[4,3,128]{2,1,0:T(4,128)S(1)}, f32[4,3,128]{2,1,0:T(4,128)S(1)}, u32[]{:S(2)}, u32[]{:S(2)}) collective-permute-start(f32[4,3,128]{2,1,0:T(4,128)S(1)} %get-tuple-element.886), channel_id=1, source_target_pairs={{16,0},{32,16},{48,32},{64,48},{80,64},{96,80},{112,96},{128,112},... | collective-permute-start | bytes 18440 | tf_op jit(solution)/shard_map/ppermute | solution.py:16
  382.9 1.9 collective-permute-start.24
  384.8 3.4 collective-permute-start.26
  388.2 4.0 collective-permute-start.28
  392.2 1.9 collective-permute-start.30
  394.2 1.9 collective-permute-start.23
  396.1 1.9 collective-permute-start.25
  398.1 1.9 collective-permute-start.27
  400.0 4.9 %collective-permute-start.29 = (f32[3,128]{1,0:T(4,128)S(1)}, f32[3,128]{1,0:T(4,128)S(1)}, u32[]{:S(2)}, u32[]{:S(2)}) collective-permute-start(f32[3,128]{1,0:T(4,128)S(1)} %collective-permute-done.28), channel_id=1, source_target_pairs={{0,1},{1,2},{2,3},{3,4},{4,5},{5,6},{6,7},{7,8},{8,9},{9,10},{10,1... | collective-permute-start | bytes 4616 | tf_op jit(solution)/shard_map/ppermute | solution.py:16
  404.9 2.4 collective-permute-start.31
  407.4 1.7 constant_dynamic-update-slice_fusion.47
  (3308 shorter events, 257.2 us)
Async XLA Ops:
  1.5 30.0 %collective-permute-start = (f32[1,4,5,128]{3,1,2,0:T(4,128)S(1)}, f32[1,4,5,128]{3,1,2,0:T(4,128)S(1)}, u32[]{:S(2)}, u32[]{:S(2)}) collective-permute-start(f32[1,4,5,128]{3,1,2,0:T(4,128)S(1)} %get-tuple-element.891), channel_id=1, source_target_pairs={{0,16},{16,32},{32,48},{48,64},{64,80},{80,96},{96,112},{112,128},... | collective-permute-start | bytes 30728 | tf_op jit(solution)/shard_map/ppermute | solution.py:24
  5.5 26.0 %collective-permute-start.1 = (f32[1,4,5,128]{3,1,2,0:T(4,128)S(1)}, f32[1,4,5,128]{3,1,2,0:T(4,128)S(1)}, u32[]{:S(2)}, u32[]{:S(2)}) collective-permute-start(f32[1,4,5,128]{3,1,2,0:T(4,128)S(1)} %get-tuple-element.892), channel_id=1, source_target_pairs={{16,0},{32,16},{48,32},{64,48},{80,64},{96,80},{112,96},{128,112},... | collective-permute-start | bytes 30728 | tf_op jit(solution)/shard_map/ppermute | solution.py:27
  18.6 12.1 %copy-start.4 = (s32[8,4,128]{2,1,0:T(4,128)S(1)}, s32[8,4,128]{2,1,0:T(4,128)}, u32[]{:S(2)}) copy-start(s32[8,4,128]{2,1,0:T(4,128)} %param.50) | copy-start | bytes 49156
  18.6 12.1 %copy-start.7 = (s32[4]{0:T(128)S(1)}, s32[4]{0:T(128)}, u32[]{:S(2)}) copy-start(s32[4]{0:T(128)} %constant.972.clone.1) | copy-start | bytes 52
  18.6 12.9 %copy-start.1 = (f32[8,4,3,128]{3,1,2,0:T(4,128)S(1)}, f32[8,4,3,128]{3,1,2,0:T(4,128)}, u32[]{:S(2)}) copy-start(f32[8,4,3,128]{3,1,2,0:T(4,128)} %param.47) | copy-start | bytes 147460
  30.7 0.8 copy-start.2
  30.7 0.8 copy-start.3
  30.7 0.8 copy-start.6
  31.6 7.5 %collective-permute-start.2 = (f32[10,1,5,128]{3,1,2,0:T(1,128)S(1)}, f32[10,1,5,128]{3,1,2,0:T(1,128)S(1)}, u32[]{:S(2)}, u32[]{:S(2)}) collective-permute-start(f32[10,1,5,128]{3,1,2,0:T(1,128)S(1)} %get-tuple-element.889), channel_id=1, source_target_pairs={{0,1},{1,2},{2,3},{3,4},{4,5},{5,6},{6,7},{7,8},{8,9},{9,10},{10,1... | collective-permute-start | bytes 76808 | tf_op jit(solution)/shard_map/ppermute | solution.py:24
  36.9 2.0 copy-start.5
  36.9 6.4 %collective-permute-start.3 = (f32[10,1,5,128]{3,1,2,0:T(1,128)S(1)}, f32[10,1,5,128]{3,1,2,0:T(1,128)S(1)}, u32[]{:S(2)}, u32[]{:S(2)}) collective-permute-start(f32[10,1,5,128]{3,1,2,0:T(1,128)S(1)} %get-tuple-element.890), channel_id=1, source_target_pairs={{1,0},{2,1},{3,2},{4,3},{5,4},{6,5},{7,6},{8,7},{9,8},{10,9},{11,1... | collective-permute-start | bytes 76808 | tf_op jit(solution)/shard_map/ppermute | solution.py:27
  173.4 15.8 %collective-permute-start.4 = (f32[8,18,128]{2,1,0:T(8,128)S(1)}, f32[8,18,128]{2,1,0:T(8,128)S(1)}, u32[]{:S(2)}, u32[]{:S(2)}) collective-permute-start(f32[8,18,128]{2,1,0:T(8,128)S(1)} %get-tuple-element.876), channel_id=1, source_target_pairs={{1,0},{2,1},{3,2},{4,3},{5,4},{6,5},{7,6},{8,7},{9,8},{10,9},{11,1... | collective-permute-start | bytes 221192 | tf_op jit(solution)/shard_map/ppermute | solution.py:16
  175.3 18.1 %collective-permute-start.5 = (f32[8,18,128]{2,1,0:T(8,128)S(1)}, f32[8,18,128]{2,1,0:T(8,128)S(1)}, u32[]{:S(2)}, u32[]{:S(2)}) collective-permute-start(f32[8,18,128]{2,1,0:T(8,128)S(1)} %get-tuple-element.875), channel_id=1, source_target_pairs={{0,1},{1,2},{2,3},{3,4},{4,5},{5,6},{6,7},{7,8},{8,9},{9,10},{10,1... | collective-permute-start | bytes 221192 | tf_op jit(solution)/shard_map/ppermute | solution.py:16
  180.2 25.9 %collective-permute-start.6 = (f32[4,18,128]{2,1,0:T(8,128)S(1)}, f32[4,18,128]{2,1,0:T(8,128)S(1)}, u32[]{:S(2)}, u32[]{:S(2)}) collective-permute-start(f32[4,18,128]{2,1,0:T(8,128)S(1)} %get-tuple-element.874), channel_id=1, source_target_pairs={{16,0},{32,16},{48,32},{64,48},{80,64},{96,80},{112,96},{128,112},... | collective-permute-start | bytes 110600 | tf_op jit(solution)/shard_map/ppermute | solution.py:16
  183.9 11.6 %collective-permute-start.8 = (f32[18,128]{1,0:T(8,128)S(1)}, f32[18,128]{1,0:T(8,128)S(1)}, u32[]{:S(2)}, u32[]{:S(2)}) collective-permute-start(f32[18,128]{1,0:T(8,128)S(1)} %get-tuple-element.872), channel_id=1, source_target_pairs={{16,0},{32,16},{48,32},{64,48},{80,64},{96,80},{112,96},{128,112},... | collective-permute-start | bytes 27656 | tf_op jit(solution)/shard_map/ppermute | solution.py:16
  186.0 11.4 %collective-permute-start.10 = (f32[18,128]{1,0:T(8,128)S(1)}, f32[18,128]{1,0:T(8,128)S(1)}, u32[]{:S(2)}, u32[]{:S(2)}) collective-permute-start(f32[18,128]{1,0:T(8,128)S(1)} %get-tuple-element.871), channel_id=1, source_target_pairs={{0,16},{16,32},{32,48},{48,64},{64,80},{80,96},{96,112},{112,128},... | collective-permute-start | bytes 27656 | tf_op jit(solution)/shard_map/ppermute | solution.py:16
  189.2 10.2 %collective-permute-start.12 = (f32[18,128]{1,0:T(8,128)S(1)}, f32[18,128]{1,0:T(8,128)S(1)}, u32[]{:S(2)}, u32[]{:S(2)}) collective-permute-start(f32[18,128]{1,0:T(8,128)S(1)} %get-tuple-element.870), channel_id=1, source_target_pairs={{16,0},{32,16},{48,32},{64,48},{80,64},{96,80},{112,96},{128,112},... | collective-permute-start | bytes 27656 | tf_op jit(solution)/shard_map/ppermute | solution.py:16
  193.5 7.8 %collective-permute-start.14 = (f32[18,128]{1,0:T(8,128)S(1)}, f32[18,128]{1,0:T(8,128)S(1)}, u32[]{:S(2)}, u32[]{:S(2)}) collective-permute-start(f32[18,128]{1,0:T(8,128)S(1)} %get-tuple-element.869), channel_id=1, source_target_pairs={{0,16},{16,32},{32,48},{48,64},{64,80},{80,96},{96,112},{112,128},... | collective-permute-start | bytes 27656 | tf_op jit(solution)/shard_map/ppermute | solution.py:16
  195.5 13.1 %collective-permute-start.7 = (f32[4,18,128]{2,1,0:T(8,128)S(1)}, f32[4,18,128]{2,1,0:T(8,128)S(1)}, u32[]{:S(2)}, u32[]{:S(2)}) collective-permute-start(f32[4,18,128]{2,1,0:T(8,128)S(1)} %get-tuple-element.873), channel_id=1, source_target_pairs={{0,16},{16,32},{32,48},{48,64},{64,80},{80,96},{96,112},{112,128},... | collective-permute-start | bytes 110600 | tf_op jit(solution)/shard_map/ppermute | solution.py:16
  197.4 11.2 %collective-permute-start.9 = (f32[18,128]{1,0:T(8,128)S(1)}, f32[18,128]{1,0:T(8,128)S(1)}, u32[]{:S(2)}, u32[]{:S(2)}) collective-permute-start(f32[18,128]{1,0:T(8,128)S(1)} %collective-permute-done.8), channel_id=1, source_target_pairs={{1,0},{2,1},{3,2},{4,3},{5,4},{6,5},{7,6},{8,7},{9,8},{10,9},{11,1... | collective-permute-start | bytes 27656 | tf_op jit(solution)/shard_map/ppermute | solution.py:16
  199.3 9.3 %collective-permute-start.11 = (f32[18,128]{1,0:T(8,128)S(1)}, f32[18,128]{1,0:T(8,128)S(1)}, u32[]{:S(2)}, u32[]{:S(2)}) collective-permute-start(f32[18,128]{1,0:T(8,128)S(1)} %collective-permute-done.10), channel_id=1, source_target_pairs={{1,0},{2,1},{3,2},{4,3},{5,4},{6,5},{7,6},{8,7},{9,8},{10,9},{11,1... | collective-permute-start | bytes 27656 | tf_op jit(solution)/shard_map/ppermute | solution.py:16
  201.3 9.1 %collective-permute-start.13 = (f32[18,128]{1,0:T(8,128)S(1)}, f32[18,128]{1,0:T(8,128)S(1)}, u32[]{:S(2)}, u32[]{:S(2)}) collective-permute-start(f32[18,128]{1,0:T(8,128)S(1)} %collective-permute-done.12), channel_id=1, source_target_pairs={{0,1},{1,2},{2,3},{3,4},{4,5},{5,6},{6,7},{7,8},{8,9},{9,10},{10,1... | collective-permute-start | bytes 27656 | tf_op jit(solution)/shard_map/ppermute | solution.py:16
  206.2 4.5 %collective-permute-start.15 = (f32[18,128]{1,0:T(8,128)S(1)}, f32[18,128]{1,0:T(8,128)S(1)}, u32[]{:S(2)}, u32[]{:S(2)}) collective-permute-start(f32[18,128]{1,0:T(8,128)S(1)} %collective-permute-done.14), channel_id=1, source_target_pairs={{0,1},{1,2},{2,3},{3,4},{4,5},{5,6},{6,7},{7,8},{8,9},{9,10},{10,1... | collective-permute-start | bytes 27656 | tf_op jit(solution)/shard_map/ppermute | solution.py:16
  212.5 7.4 %collective-permute-start.16 = (f32[1,4,9,128]{3,0,2,1:T(1,128)S(1)}, f32[1,4,9,128]{3,0,2,1:T(1,128)S(1)}, u32[]{:S(2)}, u32[]{:S(2)}) collective-permute-start(f32[1,4,9,128]{3,0,2,1:T(1,128)S(1)} %get-tuple-element.879), channel_id=1, source_target_pairs={{0,16},{16,32},{32,48},{48,64},{64,80},{80,96},{96,112},{112,128},... | collective-permute-start | bytes 55304 | tf_op jit(solution)/shard_map/ppermute | solution.py:24
  214.4 6.3 %collective-permute-start.17 = (f32[1,4,9,128]{3,0,2,1:T(1,128)S(1)}, f32[1,4,9,128]{3,0,2,1:T(1,128)S(1)}, u32[]{:S(2)}, u32[]{:S(2)}) collective-permute-start(f32[1,4,9,128]{3,0,2,1:T(1,128)S(1)} %get-tuple-element.880), channel_id=1, source_target_pairs={{16,0},{32,16},{48,32},{64,48},{80,64},{96,80},{112,96},{128,112},... | collective-permute-start | bytes 55304 | tf_op jit(solution)/shard_map/ppermute | solution.py:27
  220.8 17.1 %collective-permute-start.18 = (f32[10,1,9,128]{3,0,2,1:T(8,128)S(1)}, f32[10,1,9,128]{3,0,2,1:T(8,128)S(1)}, u32[]{:S(2)}, u32[]{:S(2)}) collective-permute-start(f32[10,1,9,128]{3,0,2,1:T(8,128)S(1)} %get-tuple-element.877), channel_id=1, source_target_pairs={{0,1},{1,2},{2,3},{3,4},{4,5},{5,6},{6,7},{7,8},{8,9},{9,10},{10,1... | collective-permute-start | bytes 138248 | tf_op jit(solution)/shard_map/ppermute | solution.py:24
  226.1 11.8 %collective-permute-start.19 = (f32[10,1,9,128]{3,0,2,1:T(8,128)S(1)}, f32[10,1,9,128]{3,0,2,1:T(8,128)S(1)}, u32[]{:S(2)}, u32[]{:S(2)}) collective-permute-start(f32[10,1,9,128]{3,0,2,1:T(8,128)S(1)} %get-tuple-element.878), channel_id=1, source_target_pairs={{1,0},{2,1},{3,2},{4,3},{5,4},{6,5},{7,6},{8,7},{9,8},{10,9},{11,1... | collective-permute-start | bytes 138248 | tf_op jit(solution)/shard_map/ppermute | solution.py:27
  238.0 0.8 copy-start
  370.0 18.2 %collective-permute-start.20 = (f32[8,3,128]{2,1,0:T(4,128)S(1)}, f32[8,3,128]{2,1,0:T(4,128)S(1)}, u32[]{:S(2)}, u32[]{:S(2)}) collective-permute-start(f32[8,3,128]{2,1,0:T(4,128)S(1)} %get-tuple-element.888), channel_id=1, source_target_pairs={{1,0},{2,1},{3,2},{4,3},{5,4},{6,5},{7,6},{8,7},{9,8},{10,9},{11,1... | collective-permute-start | bytes 36872 | tf_op jit(solution)/shard_map/ppermute | solution.py:16
  372.0 20.3 %collective-permute-start.21 = (f32[8,3,128]{2,1,0:T(4,128)S(1)}, f32[8,3,128]{2,1,0:T(4,128)S(1)}, u32[]{:S(2)}, u32[]{:S(2)}) collective-permute-start(f32[8,3,128]{2,1,0:T(4,128)S(1)} %get-tuple-element.887), channel_id=1, source_target_pairs={{0,1},{1,2},{2,3},{3,4},{4,5},{5,6},{6,7},{7,8},{8,9},{9,10},{10,1... | collective-permute-start | bytes 36872 | tf_op jit(solution)/shard_map/ppermute | solution.py:16
  376.8 28.1 %collective-permute-start.22 = (f32[4,3,128]{2,1,0:T(4,128)S(1)}, f32[4,3,128]{2,1,0:T(4,128)S(1)}, u32[]{:S(2)}, u32[]{:S(2)}) collective-permute-start(f32[4,3,128]{2,1,0:T(4,128)S(1)} %get-tuple-element.886), channel_id=1, source_target_pairs={{16,0},{32,16},{48,32},{64,48},{80,64},{96,80},{112,96},{128,112},... | collective-permute-start | bytes 18440 | tf_op jit(solution)/shard_map/ppermute | solution.py:16
  382.9 11.3 %collective-permute-start.24 = (f32[3,128]{1,0:T(4,128)S(1)}, f32[3,128]{1,0:T(4,128)S(1)}, u32[]{:S(2)}, u32[]{:S(2)}) collective-permute-start(f32[3,128]{1,0:T(4,128)S(1)} %get-tuple-element.884), channel_id=1, source_target_pairs={{16,0},{32,16},{48,32},{64,48},{80,64},{96,80},{112,96},{128,112},... | collective-permute-start | bytes 4616 | tf_op jit(solution)/shard_map/ppermute | solution.py:16
  384.8 11.3 %collective-permute-start.26 = (f32[3,128]{1,0:T(4,128)S(1)}, f32[3,128]{1,0:T(4,128)S(1)}, u32[]{:S(2)}, u32[]{:S(2)}) collective-permute-start(f32[3,128]{1,0:T(4,128)S(1)} %get-tuple-element.883), channel_id=1, source_target_pairs={{0,16},{16,32},{32,48},{48,64},{64,80},{80,96},{96,112},{112,128},... | collective-permute-start | bytes 4616 | tf_op jit(solution)/shard_map/ppermute | solution.py:16
  388.2 9.9 %collective-permute-start.28 = (f32[3,128]{1,0:T(4,128)S(1)}, f32[3,128]{1,0:T(4,128)S(1)}, u32[]{:S(2)}, u32[]{:S(2)}) collective-permute-start(f32[3,128]{1,0:T(4,128)S(1)} %get-tuple-element.882), channel_id=1, source_target_pairs={{16,0},{32,16},{48,32},{64,48},{80,64},{96,80},{112,96},{128,112},... | collective-permute-start | bytes 4616 | tf_op jit(solution)/shard_map/ppermute | solution.py:16
  392.2 7.8 %collective-permute-start.30 = (f32[3,128]{1,0:T(4,128)S(1)}, f32[3,128]{1,0:T(4,128)S(1)}, u32[]{:S(2)}, u32[]{:S(2)}) collective-permute-start(f32[3,128]{1,0:T(4,128)S(1)} %get-tuple-element.881), channel_id=1, source_target_pairs={{0,16},{16,32},{32,48},{48,64},{64,80},{80,96},{96,112},{112,128},... | collective-permute-start | bytes 4616 | tf_op jit(solution)/shard_map/ppermute | solution.py:16
  394.2 13.1 %collective-permute-start.23 = (f32[4,3,128]{2,1,0:T(4,128)S(1)}, f32[4,3,128]{2,1,0:T(4,128)S(1)}, u32[]{:S(2)}, u32[]{:S(2)}) collective-permute-start(f32[4,3,128]{2,1,0:T(4,128)S(1)} %get-tuple-element.885), channel_id=1, source_target_pairs={{0,16},{16,32},{32,48},{48,64},{64,80},{80,96},{96,112},{112,128},... | collective-permute-start | bytes 18440 | tf_op jit(solution)/shard_map/ppermute | solution.py:16
  396.1 11.2 %collective-permute-start.25 = (f32[3,128]{1,0:T(4,128)S(1)}, f32[3,128]{1,0:T(4,128)S(1)}, u32[]{:S(2)}, u32[]{:S(2)}) collective-permute-start(f32[3,128]{1,0:T(4,128)S(1)} %collective-permute-done.24), channel_id=1, source_target_pairs={{1,0},{2,1},{3,2},{4,3},{5,4},{6,5},{7,6},{8,7},{9,8},{10,9},{11,1... | collective-permute-start | bytes 4616 | tf_op jit(solution)/shard_map/ppermute | solution.py:16
  398.1 9.3 %collective-permute-start.27 = (f32[3,128]{1,0:T(4,128)S(1)}, f32[3,128]{1,0:T(4,128)S(1)}, u32[]{:S(2)}, u32[]{:S(2)}) collective-permute-start(f32[3,128]{1,0:T(4,128)S(1)} %collective-permute-done.26), channel_id=1, source_target_pairs={{1,0},{2,1},{3,2},{4,3},{5,4},{6,5},{7,6},{8,7},{9,8},{10,9},{11,1... | collective-permute-start | bytes 4616 | tf_op jit(solution)/shard_map/ppermute | solution.py:16
  400.0 9.1 %collective-permute-start.29 = (f32[3,128]{1,0:T(4,128)S(1)}, f32[3,128]{1,0:T(4,128)S(1)}, u32[]{:S(2)}, u32[]{:S(2)}) collective-permute-start(f32[3,128]{1,0:T(4,128)S(1)} %collective-permute-done.28), channel_id=1, source_target_pairs={{0,1},{1,2},{2,3},{3,4},{4,5},{5,6},{6,7},{7,8},{8,9},{9,10},{10,1... | collective-permute-start | bytes 4616 | tf_op jit(solution)/shard_map/ppermute | solution.py:16
  404.9 4.3 %collective-permute-start.31 = (f32[3,128]{1,0:T(4,128)S(1)}, f32[3,128]{1,0:T(4,128)S(1)}, u32[]{:S(2)}, u32[]{:S(2)}) collective-permute-start(f32[3,128]{1,0:T(4,128)S(1)} %collective-permute-done.30), channel_id=1, source_target_pairs={{0,1},{1,2},{2,3},{3,4},{4,5},{5,6},{6,7},{7,8},{8,9},{9,10},{10,1... | collective-permute-start | bytes 4616 | tf_op jit(solution)/shard_map/ppermute | solution.py:16
where the time goes:
time: 411 us; the launch traced here: 410 us
  matrix products  131 us (32%)
  local copies, waits for them, and re-layouts  111 us (27%)
  starting transfers between devices  110 us (27%)
  other arithmetic  29.2 us (7%)
  loops' own time  21.2 us (5%)
  waiting for transfers between devices  5.11 us (1%)
    ppermute x24, starting transfers between devices, from_behind(): return lax.ppermute(array, axis, pairs)  72 us
    dot_general x40, matrix products, tile_terms(): sums_a = jnp.einsum('gcj,gij->gci', feat_b, weights, precision=highest)  50.9 us
    dot_general x40, matrix products, tile_terms(): sums_b = jnp.einsum('gci,gij->gcj', feat_a, weights, precision=highest)  35.8 us
    gather x40, local copies, waits for them, and re-layouts, one_group(): map_first, map_second = (flat_map[first_block], flat_map[second_block])  23.4 us
    gather x40, local copies, waits for them, and re-layouts, one_group(): flat_pack[second_block]  22.2 us
    gather x40, local copies, waits for them, and re-layouts, one_group(): flat_pack[first_block]  22.2 us
    ppermute x4, starting transfers between devices, with_halo(): lax.ppermute(lax.slice_in_dim(block, 0, width, axis=dim), axis, backward)  22 us
    another operation x2, loops' own time, pair_sums(): lax.scan(one_group, jnp.zeros((blocks, comp_width * points), jnp.float32)...  17.9 us
  transfers between devices with their start and end apart: 32, of which 2 were waited for; matrix products, arithmetic and copies ran while one was open for 6% of the time, Pallas kernels for 0%

commit v1 on v0

v1 whole, which is shorter than its diff:
```python
import jax
import jax.numpy as jnp
from jax import lax
from jax.experimental import pallas as pl
from jax.experimental.pallas import tpu as pltpu
from jax.sharding import PartitionSpec as P

MESH = pl.DeviceIdType.MESH
LANES = 128
BXN, BYN = 8, 4
LAME, SHEAR = 24.0, 16.0
COLUMNS = {}
for _dy in range(-3, 4):
    for _dz in range(-3, 4):
        _rest = 9 - _dy * _dy - _dz * _dz
        if _rest >= 0:
            COLUMNS[(_dy, _dz)] = max(k for k in range(4) if k * k <= _rest)
W_AT, _n = {}, 0
for _key, _m in COLUMNS.items():
    W_AT[_key] = _n
    _n += 2 * _m + 1
W_COUNT = _n
X_SLOTS = ((-1, 0), (-1, 1), (-1, -1), (1, 0), (1, 1), (1, -1))


def direction(cx, cy):
    q = 3 * cx + cy
    return q - 1 if q > 0 else 3 - q


def iota(axis):
    return lax.broadcasted_iota(jnp.int32, (8, LANES), axis)


def take(tile, index):
    return jnp.take_along_axis(tile, index, axis=1, mode="promise_in_bounds")


def lane_roll(array, by):
    by = by % LANES
    return array if by == 0 else pltpu.roll(array, by, axis=array.ndim - 1)


def row_roll(tile, by):
    return pltpu.roll(tile, by % 8, axis=0)


def inverse_of(m):
    c00 = m[4] * m[8] - m[5] * m[7]
    c01 = m[5] * m[6] - m[3] * m[8]
    c02 = m[3] * m[7] - m[4] * m[6]
    c10 = m[2] * m[7] - m[1] * m[8]
    c11 = m[0] * m[8] - m[2] * m[6]
    c12 = m[1] * m[6] - m[0] * m[7]
    c20 = m[1] * m[5] - m[2] * m[4]
    c21 = m[2] * m[3] - m[0] * m[5]
    c22 = m[0] * m[4] - m[1] * m[3]
    scale = 1.0 / (m[0] * c00 + m[1] * c01 + m[2] * c02)
    return [c * scale for c in (c00, c10, c20, c01, c11, c21, c02, c12, c22)]


def product(a, b):
    return [
        a[3 * r] * b[c] + a[3 * r + 1] * b[3 + c] + a[3 * r + 2] * b[6 + c]
        for r in range(3)
        for c in range(3)
    ]


def times(k, value):
    return value if k == 1 else (-value if k == -1 else float(k) * value)


def add(total, value):
    return value if total is None else total + value


def extend(own, low_row, high_row, row, s):
    if s < 0:
        return jnp.where(row == 0, low_row(s + 4), row_roll(own[s + 4], 1))
    if s > 3:
        return jnp.where(row == 7, high_row(s - 4), row_roll(own[s - 4], -1))
    return own[s]


def kernel(
    disp, vol, hea, dam, pairs, dg_out, force_out,
    ysend, yrecv, xsend, xrecv, ysend2, yrecv2, xsend2, xrecv2,
    fields, own_u, health_m, weights, sums, ystress, xstress, force,
    ssem, rsem, ssem2, rsem2,
):
    n_gx, n_gy = lax.axis_size("gx"), lax.axis_size("gy")
    me_x, me_y = lax.axis_index("gx"), lax.axis_index("gy")

    def device(cx, cy):
        return (lax.rem(me_x + (cx + n_gx), n_gx), lax.rem(me_y + (cy + n_gy), n_gy))

    barrier = pltpu.get_barrier_semaphore()
    for cx in (-1, 0, 1):
        for cy in (-1, 0, 1):
            if cx or cy:
                pl.semaphore_signal(barrier, inc=1, device_id=device(cx, cy), device_id_type=MESH)

    row, lane = iota(0), iota(1)
    block_y, y_in, z_at = lane // 32, (lane // 8) % 4, lane % 8
    y_at = lane // 8

    ax, ay, bx, by = (pairs[i : i + 1, :] for i in range(4))
    q = 3 * (bx - ax) + (by - ay) - 1
    wide = lax.broadcasted_iota(jnp.int32, (LANES, 256), 0)
    tall = lax.broadcasted_iota(jnp.int32, (8, 256), 0)
    flags = None
    for at_x, at_y, way in ((ax, ay, q), (bx, by, q + 4)):
        in_row = jnp.where(tall == at_x - 1, 1.0, 0.0)
        in_lane = jnp.where(wide == 8 * at_y + way, 1.0, 0.0)
        flags = add(flags, lax.dot_general(
            in_row, in_lane, (((1,), (1,)), ((), ())), preferred_element_type=jnp.float32))

    to_x = [16 * z_at + 4 * y_in + t for t in range(4)]
    raw = []
    for b in range(BYN):
        v = vol[:, b, :]
        raw.append([hea[:, b, :], v] + [v * disp[:, b, c, :] for c in range(3)])
    u_raw = [[disp[:, b, c, :] for b in range(BYN)] for c in range(3)]

    def lattice_tile(of_block, t):
        got = take(of_block[0], to_x[t])
        for b in range(1, BYN):
            got = jnp.where(block_y == b, take(of_block[b], to_x[t]), got)
        return got

    own = []
    for f in range(5):
        ysend[0, f] = raw[0][f]
        ysend[1, f] = raw[3][f]
        own.append([lattice_tile([raw[b][f] for b in range(BYN)], t) for t in range(4)])
        for t in range(3):
            xsend[0, 3 * f + t : 3 * f + t + 1, :] = own[f][t][0:1]
            xsend[1, 3 * f + t : 3 * f + t + 1, :] = own[f][t + 1][7:8]
    ysend[0, 5] = flags
    ysend[1, 5] = flags
    xsend[0, 15:16, :] = flags[0:1]
    xsend[1, 15:16, :] = flags[7:8]
    pl.semaphore_wait(barrier, 8)

    def exchange(x_src, x_dst, y_src, y_dst, sends, recvs):
        copies = []
        for n, (cx, cy) in enumerate(X_SLOTS):
            copies.append(pltpu.make_async_remote_copy(
                src_ref=x_src.at[0 if cx == 1 else 1], dst_ref=x_dst.at[n],
                send_sem=sends.at[n], recv_sem=recvs.at[n],
                device_id=device(-cx, -cy), device_id_type=MESH))
        for n, cy in enumerate((1, -1)):
            copies.append(pltpu.make_async_remote_copy(
                src_ref=y_src.at[n], dst_ref=y_dst.at[n],
                send_sem=sends.at[6 + n], recv_sem=recvs.at[6 + n],
                device_id=device(0, -cy), device_id_type=MESH))
        for copy in copies:
            copy.start()
        return copies

    copies = exchange(xsend, xrecv, ysend, yrecv, ssem, rsem)

    for c in range(3):
        for t in range(4):
            own_u[c, t] = lattice_tile(u_raw[c], t)
    for copy in copies:
        copy.wait_recv()

    def flag_ext(tile, slots, cx):
        if cx == 0:
            return tile
        r = xrecv[slots[cx], 15:16, :]
        if cx < 0:
            return jnp.where(row == 0, r, row_roll(tile, 1))
        return jnp.where(row == 7, r, row_roll(tile, -1))

    seen = {}
    for cy, tile, slots in (
        (0, flags, {-1: 0, 1: 3}), (1, yrecv[0, 5], {-1: 1, 1: 4}), (-1, yrecv[1, 5], {-1: 2, 1: 5})
    ):
        for cx in (-1, 0, 1):
            seen[(cx, cy)] = flag_ext(tile, slots, cx)
    enabled = {}
    for cx in (-1, 0, 1):
        for cy in (-1, 0, 1):
            if cx == 0 and cy == 0:
                continue
            mine = take(flags, 8 * (block_y + 1) + direction(cx, cy))
            back = direction(-cx, -cy)
            theirs = take(seen[(cx, 0)], 8 * (block_y + cy + 1) + back)
            if cy == 1:
                theirs = jnp.where(block_y == 3, take(seen[(cx, 1)], 8 + back + 0 * lane), theirs)
            if cy == -1:
                theirs = jnp.where(block_y == 0, take(seen[(cx, -1)], 32 + back + 0 * lane), theirs)
            enabled[(cx, cy)] = jnp.minimum(jnp.maximum(mine, theirs), 1.0)

    for dy in range(-3, 4):
        deep = max(m for (a, _), m in COLUMNS.items() if a == dy)
        by_cx = {}
        for cx in (-1, 0, 1):
            near = enabled.get((cx, 0))
            if dy > 0:
                far = enabled[(cx, 1)]
                near = 1.0 if near is None else near
                by_cx[cx] = jnp.where(y_in + dy >= 4, far, near)
            elif dy < 0:
                far = enabled[(cx, -1)]
                near = 1.0 if near is None else near
                by_cx[cx] = jnp.where(y_in + dy < 0, far, near)
            else:
                by_cx[cx] = near
        for dx in range(-deep, deep + 1):
            for t in range(4):
                cx = (t + dx) // 4
                h = own[0][t]
                health_m[dy + 3, dx + 3, t] = h if by_cx[cx] is None else h * by_cx[cx]

    side_lane = lane < 64
    side = y_at < 8
    for f in range(5):
        beside = []
        for t in range(4):
            beside.append(jnp.where(side, take(yrecv[0, f], to_x[t]), take(yrecv[1, f], to_x[t])))

        def row_at(slot, t, f=f):
            return xrecv[slot, 3 * f + t : 3 * f + t + 1, :]

        def corner(low, high, t, f=f):
            return jnp.where(side_lane[0:1], row_at(low, t, f), row_at(high, t, f))

        for s in range(-3, 7):
            inner = extend(own[f], lambda t: row_at(0, t - 1), lambda t: row_at(3, t), row, s)
            fields[3, f, s + 3] = inner
            if s < -2 or s > 5:
                continue
            outer = extend(beside, lambda t: corner(1, 2, t - 1), lambda t: corner(4, 5, t), row, s)
            for k in (1, 2, 3):
                if k == 3 and not 0 <= s <= 3:
                    continue
                fields[3 + k, f, s + 3] = jnp.where(y_at < k, outer, inner)
                fields[3 - k, f, s + 3] = jnp.where(y_at >= 16 - k, outer, inner)

    z_ok = {dz: (z_at + dz >= 0) & (z_at + dz < 8) for dz in range(-3, 4)}

    def first_sums(half, carry):
        base = 2 * half
        total = {}
        for dy in range(-3, 4):
            part = {}
            for dz in range(-3, 4):
                if (dy, dz) not in COLUMNS:
                    continue
                deep = COLUMNS[(dy, dz)]
                turn = -(8 * dy + dz)
                src = [
                    lane_roll(fields[dy + 3, f, pl.ds(base + 3 - deep, 2 + 2 * deep)], turn)
                    for f in range(5)
                ]
                if dz != 0:
                    src[0] = jnp.where(z_ok[dz][None], src[0], 0.0)
                a0, a1, a2 = [None] * 4, [None] * 4, None
                for reach in range(deep + 1):
                    terms = []
                    for dx in (reach, -reach) if reach else (0,):
                        lo = deep + dx
                        w = jnp.minimum(
                            health_m[dy + 3, dx + 3, pl.ds(base, 2)], src[0][lo : lo + 2])
                        weights[W_AT[(dy, dz)] + lo, pl.ds(base, 2)] = w
                        if dy == 0 and dz == 0 and dx == 0:
                            continue
                        terms.append([w * src[k + 1][lo : lo + 2] for k in range(4)])
                    if not terms:
                        continue
                    for k in range(4):
                        both = terms[0][k] if reach == 0 else terms[0][k] + terms[1][k]
                        a0[k] = add(a0[k], both)
                        if reach:
                            a1[k] = add(a1[k], times(reach, terms[0][k] - terms[1][k]))
                            if k == 0:
                                a2 = add(a2, times(reach * reach, both))
                for k in range(4):
                    if dy != 0:
                        part["y", k] = add(part.get(("y", k)), a0[k])
                    if dz != 0:
                        part["z", k] = add(part.get(("z", k)), times(dz, a0[k]))
                    if a1[k] is not None:
                        part["x", k] = add(part.get(("x", k)), a1[k])
                if dz != 0:
                    part["zz"] = add(part.get("zz"), times(dz * dz, a0[0]))
                    if a1[0] is not None:
                        part["xz"] = add(part.get("xz"), times(dz, a1[0]))
                if a2 is not None:
                    part["xx"] = add(part.get("xx"), a2)
            for k in range(4):
                if dy != 0:
                    total["y", k] = add(total.get(("y", k)), times(dy, part["y", k]))
                for name in ("x", "z"):
                    if (name, k) in part:
                        total[name, k] = add(total.get((name, k)), part[name, k])
            if dy != 0:
                total["yy"] = add(total.get("yy"), times(dy * dy, part["y", 0]))
                for name, to in (("x", "xy"), ("z", "yz")):
                    if (name, 0) in part:
                        total[to] = add(total.get(to), times(dy, part[name, 0]))
            for name in ("xx", "zz", "xz"):
                if name in part:
                    total[name] = add(total.get(name), part[name])
        order = ["xx", "xy", "xz", "yy", "yz", "zz"] + [(a, k) for k in range(4) for a in "xyz"]
        for n, name in enumerate(order):
            sums[n, pl.ds(base, 2)] = total[name]
        return carry

    lax.fori_loop(0, 2, first_sums, 0)

    dam_raw = [dam[:, b, :].astype(jnp.float32) for b in range(BYN)]
    to_raw = [8 * (4 * b + (lane // 4) % 4) + lane // 16 for b in range(BYN)]
    x_in = lane % 4

    def block_tile(of_x, b):
        got = take(of_x[0], to_raw[b])
        for t in range(1, 4):
            got = jnp.where(x_in == t, take(of_x[t], to_raw[b]), got)
        return got

    deform, stress = [], []
    for t in range(4):
        kxx, kxy, kxz, kyy, kyz, kzz = (sums[n, t] for n in range(6))
        span = [sums[6 + n, t] for n in range(3)]
        sym = [kxx, kxy, kxz, kxy, kyy, kyz, kxz, kyz, kzz]
        moment = [
            sym[3 * c + d] + sums[9 + 3 * c + d, t] - own_u[c, t] * span[d]
            for c in range(3) for d in range(3)
        ]
        shape = [sym[n] + 1.0 if n % 4 == 0 else sym[n] for n in range(9)]
        inv = inverse_of(shape)
        grad = product(moment, inv)
        flip = [grad[3 * (n % 3) + n // 3] for n in range(9)]
        twice = product(flip, grad)
        strain = [0.5 * (twice[n] - 1.0) if n % 4 == 0 else 0.5 * twice[n] for n in range(9)]
        trace = LAME * (strain[0] + strain[4] + strain[8])
        second = [
            trace + 2.0 * SHEAR * strain[n] if n % 4 == 0 else 2.0 * SHEAR * strain[n]
            for n in range(9)
        ]
        intact = 1.0 - lattice_tile(dam_raw, t)
        first = [e * intact for e in product(grad, second)]
        mapped = product(first, inv)
        for c in range(3):
            force[c, t] = mapped[3 * c] * span[0] + mapped[3 * c + 1] * span[1] + mapped[3 * c + 2] * span[2]
        v = own[1][t]
        deform.append(grad)
        stress.append([v * e for e in mapped])

    for n in range(9):
        of_x = [stress[t][n] for t in range(4)]
        for t in range(3):
            xsend2[0, 3 * n + t : 3 * n + t + 1, :] = of_x[t][0:1]
            xsend2[1, 3 * n + t : 3 * n + t + 1, :] = of_x[t + 1][7:8]
        low = of_x[0]
        high = lane_roll(of_x[0], 32)
        for t in range(1, 4):
            low = jnp.where(block_y == t, lane_roll(of_x[t], 32 * t), low)
            high = jnp.where(block_y == t, lane_roll(of_x[t], 32 * (t - 3)), high)
        ysend2[0, n] = low
        ysend2[1, n] = high
        for t in range(4):
            xstress[n, t] = of_x[t]

    copies2 = exchange(xsend2, xrecv2, ysend2, yrecv2, ssem2, rsem2)

    for n in range(9):
        for b in range(BYN):
            dg_out[b, n] = block_tile([deform[t][n] for t in range(4)], b)
    for copy in copies2:
        copy.wait_recv()

    for n in range(9):
        mine = [xstress[n, t] for t in range(4)]
        beside = []
        for t in range(4):
            beside.append(jnp.where(
                side, lane_roll(yrecv2[0, n], -32 * t), lane_roll(yrecv2[1, n], 32 * (3 - t))))

        def row_at2(slot, t, n=n):
            return xrecv2[slot, 3 * n + t : 3 * n + t + 1, :]

        def corner2(low, high, t):
            return jnp.where(side_lane[0:1], row_at2(low, t), row_at2(high, t))

        for s in range(-3, 7):
            inner = extend(mine, lambda t: row_at2(0, t - 1), lambda t: row_at2(3, t), row, s)
            ystress[3, n, s + 3] = inner
            if s < -2 or s > 5:
                continue
            outer = extend(beside, lambda t: corner2(1, 2, t - 1), lambda t: corner2(4, 5, t), row, s)
            for k in (1, 2, 3):
                if k == 3 and not 0 <= s <= 3:
                    continue
                ystress[3 + k, n, s + 3] = jnp.where(y_at < k, outer, inner)
                ystress[3 - k, n, s + 3] = jnp.where(y_at >= 16 - k, outer, inner)

    def second_sums(c, carry):
        total = force[c]
        for dy in range(-3, 4):
            for dz in range(-3, 4):
                if (dy, dz) not in COLUMNS:
                    continue
                deep = COLUMNS[(dy, dz)]
                turn = -(8 * dy + dz)
                tiles = pl.ds(3 - deep, 4 + 2 * deep)
                fixed = None
                if dy != 0:
                    fixed = add(fixed, times(dy, ystress[dy + 3, 3 * c + 1, tiles]))
                if dz != 0:
                    fixed = add(fixed, times(dz, ystress[dy + 3, 3 * c + 2, tiles]))
                if fixed is not None:
                    fixed = lane_roll(fixed, turn)
                slope = lane_roll(ystress[dy + 3, 3 * c, tiles], turn) if deep else None
                for dx in range(-deep, deep + 1):
                    lo = deep + dx
                    value = None if fixed is None else fixed[lo : lo + 4]
                    if dx != 0:
                        value = add(value, times(dx, slope[lo : lo + 4]))
                    if value is not None:
                        total = total + weights[W_AT[(dy, dz)] + lo] * value
        force[c] = total
        return carry

    lax.fori_loop(0, 3, second_sums, 0)
    for c in range(3):
        for b in range(BYN):
            force_out[b, c] = block_tile([force[c, t] for t in range(4)], b)
    for copy in copies + copies2:
        copy.wait_send()


def local(displacement, volume, health, damage, block_pairs):
    pairs = jnp.pad(block_pairs[0, 0].T, ((0, 0), (0, 256 - block_pairs.shape[2])), constant_values=-1)
    f32 = jnp.float32
    vmem = pl.BlockSpec(memory_space=pltpu.VMEM)
    dg, force = pl.pallas_call(
        kernel,
        out_shape=(
            jax.ShapeDtypeStruct((BYN, 9, BXN, LANES), f32),
            jax.ShapeDtypeStruct((BYN, 3, BXN, LANES), f32),
        ),
        in_specs=[vmem] * 5,
        out_specs=(vmem, vmem),
        scratch_shapes=[
            pltpu.VMEM((2, 6, 8, LANES), f32),
            pltpu.VMEM((2, 6, 8, LANES), f32),
            pltpu.VMEM((2, 16, LANES), f32),
            pltpu.VMEM((6, 16, LANES), f32),
            pltpu.VMEM((2, 9, 8, LANES), f32),
            pltpu.VMEM((2, 9, 8, LANES), f32),
            pltpu.VMEM((2, 32, LANES), f32),
            pltpu.VMEM((6, 32, LANES), f32),
            pltpu.VMEM((7, 5, 10, 8, LANES), f32),
            pltpu.VMEM((3, 4, 8, LANES), f32),
            pltpu.VMEM((7, 7, 4, 8, LANES), f32),
            pltpu.VMEM((W_COUNT, 4, 8, LANES), f32),
            pltpu.VMEM((18, 4, 8, LANES), f32),
            pltpu.VMEM((7, 9, 10, 8, LANES), f32),
            pltpu.VMEM((9, 4, 8, LANES), f32),
            pltpu.VMEM((3, 4, 8, LANES), f32),
            pltpu.SemaphoreType.DMA((8,)),
            pltpu.SemaphoreType.DMA((8,)),
            pltpu.SemaphoreType.DMA((8,)),
            pltpu.SemaphoreType.DMA((8,)),
        ],
        compiler_params=pltpu.CompilerParams(collective_id=0, has_side_effects=True),
        name="peridynamics",
    )(displacement, volume, health, damage, pairs)
    return jnp.transpose(dg, (2, 0, 1, 3)), jnp.transpose(force, (2, 0, 1, 3))


def solution(mesh):
    in_specs = (
        P("gx", "gy", None, None),
        P("gx", "gy", None),
        P("gx", "gy", None),
        P("gx", "gy", None),
        P("gx", "gy", None, None),
    )
    out_specs = (P("gx", "gy", None, None), P("gx", "gy", None, None))
    return jax.shard_map(local, mesh=mesh, in_specs=in_specs, out_specs=out_specs, check_vma=False)
```

time: 411 us -> 40.2 us (0.10)
  the two profiles are of different devices: /device:TPU:31 before, /device:TPU:25 now
where the time goes in v1:
time: 40.2 us; the launch traced here: 39.9 us
  Pallas kernels  34.3 us (85%)
  local copies, waits for them, and re-layouts  4.99 us (12%)
  between operations  0.65 us (2%)
    pallas_call x1, Pallas kernels, local(): pl.pallas_call(kernel, out_shape=(jax.ShapeDtypeStruct((BYN, 9, BXN, LANE...  34.3 us
    unnamed x5, local copies, waits for them, and re-layouts  3.7 us
    pad x1, local copies, waits for them, and re-layouts, local(): jnp.pad(block_pairs[0, 0].T, ((0, 0), (0, 256 - block_pairs.shape[2])), c...  1.29 us

profile of v1, /device:TPU:25, one launch (start us, length us, event | category | flops | bytes accessed | tf_op | source)
XLA Modules:
  0.0 39.9 jit_solution(599654515548851064)
XLA Ops:
  0.6 1.3 %pad.4.pairs = s32[4,256]{1,0:T(4,128)} pad(s32[4,162]{1,0:T(4,128)} %bitcast.7, s32[]{:T(128)} %constant.0.clone.1), padding=0_0x0_94 | pad | bytes 6692 | tf_op jit(solution)/shard_map/jit(_pad)/pad | solution.py:439
  1.9 1.4 %copy.7.disp = f32[8,4,3,128]{3,2,1,0:T(4,128)} copy(f32[8,4,3,128]{3,1,2,0:T(4,128)} %param.5) | data formatting | bytes 98304 | tf_op args[0]
  3.4 34.3 %peridynamics.1 = (f32[4,9,8,128]{3,2,1,0:T(8,128)}, f32[4,3,8,128]{3,2,1,0:T(8,128)}) custom-call(f32[8,4,3,128]{3,2,1,0:T(4,128)} %copy.7.disp, f32[8,4,128]{2,1,0:T(4,128)} %vol.1, f32[8,4,128]{2,1,0:T(4,128)} %hea.1, s32[8,4,128]{2,1,0:T(4,128)} %dam.1, s32[4,256]{1,0:T(4,128)} %pad.4.pairs), custom_call_target="tpu_custom_call" | custom-call | tf_op jit(solution)/shard_map/peridynamics/pallas_call | solution.py:442
  37.6 0.0 copy-start
  37.6 1.6 %copy.8 = f32[8,4,9,128]{3,1,2,0:T(4,128)} copy(f32[8,4,9,128]{3,0,2,1:T(8,128)} %bitcast.5) | data formatting | bytes 294912
  39.3 0.0 copy-done
  39.3 0.6 %copy.9 = f32[8,4,3,128]{3,1,2,0:T(4,128)} copy(f32[8,4,3,128]{3,0,2,1:T(8,128)S(1)} %bitcast.6) | data formatting | bytes 98304
Async XLA Ops:
  37.6 1.6 %copy-start = (f32[4,3,8,128]{3,2,1,0:T(8,128)S(1)}, f32[4,3,8,128]{3,2,1,0:T(8,128)}, u32[]{:S(2)}) copy-start(f32[4,3,8,128]{3,2,1,0:T(8,128)} %get-tuple-element.5) | copy-start | bytes 147460

commit v2 on v1

--- a/solution.py
+++ b/solution.py
@@ -20,7 +20,7 @@
     W_AT[_key] = _n
     _n += 2 * _m + 1
 W_COUNT = _n
-X_SLOTS = ((-1, 0), (-1, 1), (-1, -1), (1, 0), (1, 1), (1, -1))
+CORNERS = ((-1, 1), (-1, -1), (1, 1), (1, -1))
 
 
 def direction(cx, cy):
@@ -84,11 +84,20 @@
 
 
 def kernel(
-    disp, vol, hea, dam, pairs, dg_out, force_out,
-    ysend, yrecv, xsend, xrecv, ysend2, yrecv2, xsend2, xrecv2,
+    disp_in, vol_in, hea_in, dam_in, pairs_in, dg_out, force_out,
+    disp, vol, hea, dam, pairs,
+    ysend, yrecv, xsend, xrecv, csend, crecv,
+    ysend2, yrecv2, xsend2, xrecv2, csend2, crecv2,
     fields, own_u, health_m, weights, sums, ystress, xstress, force,
-    ssem, rsem, ssem2, rsem2,
+    isem, ssem, rsem, ssem2, rsem2,
 ):
+    loads = [
+        pltpu.make_async_copy(src, dst, isem.at[n])
+        for n, (src, dst) in enumerate((
+            (pairs_in, pairs), (disp_in, disp), (vol_in, vol), (hea_in, hea), (dam_in, dam)))
+    ]
+    for load in loads:
+        load.start()
     n_gx, n_gy = lax.axis_size("gx"), lax.axis_size("gy")
     me_x, me_y = lax.axis_index("gx"), lax.axis_index("gy")
 
@@ -105,10 +114,13 @@
     block_y, y_in, z_at = lane // 32, (lane // 8) % 4, lane % 8
     y_at = lane // 8
 
+    for load in loads:
+        load.wait()
+    slots = pairs.shape[1]
     ax, ay, bx, by = (pairs[i : i + 1, :] for i in range(4))
     q = 3 * (bx - ax) + (by - ay) - 1
-    wide = lax.broadcasted_iota(jnp.int32, (LANES, 256), 0)
-    tall = lax.broadcasted_iota(jnp.int32, (8, 256), 0)
+    wide = lax.broadcasted_iota(jnp.int32, (LANES, slots), 0)
+    tall = lax.broadcasted_iota(jnp.int32, (8, slots), 0)
     flags = None
     for at_x, at_y, way in ((ax, ay, q), (bx, by, q + 4)):
         in_row = jnp.where(tall == at_x - 1, 1.0, 0.0)
@@ -116,12 +128,53 @@
         flags = add(flags, lax.dot_general(
             in_row, in_lane, (((1,), (1,)), ((), ())), preferred_element_type=jnp.float32))
 
-    to_x = [16 * z_at + 4 * y_in + t for t in range(4)]
+    def u_tile(c, b):
+        return disp[pl.ds(4 * c + b, 8, stride=12), :]
+
+    def row_tile(array, b):
+        return array[pl.ds(b, 8, stride=4), :]
+
     raw = []
     for b in range(BYN):
-        v = vol[:, b, :]
-        raw.append([hea[:, b, :], v] + [v * disp[:, b, c, :] for c in range(3)])
-    u_raw = [[disp[:, b, c, :] for b in range(BYN)] for c in range(3)]
+        v = row_tile(vol, b)
+        raw.append([row_tile(hea, b), v] + [v * u_tile(c, b) for c in range(3)])
+    for n, b in enumerate((0, 3)):
+        for f in range(5):
+            ysend[n, f] = raw[b][f]
+            for m, r in enumerate((0, 7)):
+                csend[2 * m + n, f : f + 1, :] = raw[b][f][r : r + 1]
+        ysend[n, 5] = flags
+        for m, r in enumerate((0, 7)):
+            csend[2 * m + n, 5:6, :] = flags[r : r + 1]
+    for m, r in enumerate((0, 7)):
+        xsend[m, 0:12, :] = disp[12 * r : 12 * r + 12, :]
+        xsend[m, 12:16, :] = vol[4 * r : 4 * r + 4, :]
+        xsend[m, 16:20, :] = hea[4 * r : 4 * r + 4, :]
+        xsend[m, 20:21, :] = flags[r : r + 1]
+    pl.semaphore_wait(barrier, 8)
+
+    def exchange(x_pair, y_pair, c_pair, sends, recvs):
+        moves = []
+        for n, cx in enumerate((-1, 1)):
+            moves.append((x_pair[0].at[1 - n], x_pair[1].at[n], -cx, 0))
+        for n, cy in enumerate((1, -1)):
+            moves.append((y_pair[0].at[n], y_pair[1].at[n], 0, -cy))
+        for n, (cx, cy) in enumerate(CORNERS):
+            at = 2 * (0 if cx == 1 else 1) + (0 if cy == 1 else 1)
+            moves.append((c_pair[0].at[at], c_pair[1].at[n], -cx, -cy))
+        copies = [
+            pltpu.make_async_remote_copy(
+                src_ref=src, dst_ref=dst, send_sem=sends.at[n], recv_sem=recvs.at[n],
+                device_id=device(tx, ty), device_id_type=MESH)
+            for n, (src, dst, tx, ty) in enumerate(moves)
+        ]
+        for copy in copies:
+            copy.start()
+        return copies
+
+    copies = exchange((xsend, xrecv), (ysend, yrecv), (csend, crecv), ssem, rsem)
+
+    to_x = [16 * z_at + 4 * y_in + t for t in range(4)]
 
     def lattice_tile(of_block, t):
         got = take(of_block[0], to_x[t])
@@ -129,58 +182,30 @@
             got = jnp.where(block_y == b, take(of_block[b], to_x[t]), got)
         return got
 
-    own = []
-    for f in range(5):
-        ysend[0, f] = raw[0][f]
-        ysend[1, f] = raw[3][f]
-        own.append([lattice_tile([raw[b][f] for b in range(BYN)], t) for t in range(4)])
-        for t in range(3):
-            xsend[0, 3 * f + t : 3 * f + t + 1, :] = own[f][t][0:1]
-            xsend[1, 3 * f + t : 3 * f + t + 1, :] = own[f][t + 1][7:8]
-    ysend[0, 5] = flags
-    ysend[1, 5] = flags
-    xsend[0, 15:16, :] = flags[0:1]
-    xsend[1, 15:16, :] = flags[7:8]
-    pl.semaphore_wait(barrier, 8)
-
-    def exchange(x_src, x_dst, y_src, y_dst, sends, recvs):
-        copies = []
-        for n, (cx, cy) in enumerate(X_SLOTS):
-            copies.append(pltpu.make_async_remote_copy(
-                src_ref=x_src.at[0 if cx == 1 else 1], dst_ref=x_dst.at[n],
-                send_sem=sends.at[n], recv_sem=recvs.at[n],
-                device_id=device(-cx, -cy), device_id_type=MESH))
-        for n, cy in enumerate((1, -1)):
-            copies.append(pltpu.make_async_remote_copy(
-                src_ref=y_src.at[n], dst_ref=y_dst.at[n],
-                send_sem=sends.at[6 + n], recv_sem=recvs.at[6 + n],
-                device_id=device(0, -cy), device_id_type=MESH))
-        for copy in copies:
-            copy.start()
-        return copies
-
-    copies = exchange(xsend, xrecv, ysend, yrecv, ssem, rsem)
-
-    for c in range(3):
-        for t in range(4):
-            own_u[c, t] = lattice_tile(u_raw[c], t)
+    own = [[lattice_tile([raw[b][f] for b in range(BYN)], t) for t in range(4)] for f in range(5)]
+    dam_raw = [row_tile(dam, b).astype(jnp.float32) for b in range(BYN)]
+    for t in range(4):
+        for c in range(3):
+            own_u[c, t] = lattice_tile([u_tile(c, b) for b in range(BYN)], t)
+        own_u[3, t] = 1.0 - lattice_tile(dam_raw, t)
     for copy in copies:
         copy.wait_recv()
 
-    def flag_ext(tile, slots, cx):
+    def flag_ext(tile, low, high, cx):
         if cx == 0:
             return tile
-        r = xrecv[slots[cx], 15:16, :]
         if cx < 0:
-            return jnp.where(row == 0, r, row_roll(tile, 1))
-        return jnp.where(row == 7, r, row_roll(tile, -1))
+            return jnp.where(row == 0, low, row_roll(tile, 1))
+        return jnp.where(row == 7, high, row_roll(tile, -1))
 
     seen = {}
-    for cy, tile, slots in (
-        (0, flags, {-1: 0, 1: 3}), (1, yrecv[0, 5], {-1: 1, 1: 4}), (-1, yrecv[1, 5], {-1: 2, 1: 5})
+    for cy, tile, low, high in (
+        (0, flags, xrecv[0, 20:21, :], xrecv[1, 20:21, :]),
+        (1, yrecv[0, 5], crecv[0, 5:6, :], crecv[2, 5:6, :]),
+        (-1, yrecv[1, 5], crecv[1, 5:6, :], crecv[3, 5:6, :]),
     ):
         for cx in (-1, 0, 1):
-            seen[(cx, cy)] = flag_ext(tile, slots, cx)
+            seen[(cx, cy)] = flag_ext(tile, low, high, cx)
     enabled = {}
     for cx in (-1, 0, 1):
         for cy in (-1, 0, 1):
@@ -217,24 +242,34 @@
                 health_m[dy + 3, dx + 3, t] = h if by_cx[cx] is None else h * by_cx[cx]
 
     side_lane = lane < 64
-    side = y_at < 8
+    edge = [
+        jnp.concatenate([xrecv[0, 4 * k : 4 * k + 4, :], xrecv[1, 4 * k : 4 * k + 4, :]], axis=0)
+        for k in (4, 3, 0, 1, 2)
+    ]
+    edge = edge[:2] + [edge[1] * e for e in edge[2:]]
+
+    def edge_tile(f, t):
+        got = jnp.where(row % 4 == block_y, take(edge[f], to_x[t]), 0.0)
+        got = got + jnp.where(row % 2 == 0, row_roll(got, -1), row_roll(got, 1))
+        return got + jnp.where(row % 4 < 2, row_roll(got, -2), row_roll(got, 2))
+
+    corner_low = [
+        jnp.where(side_lane, take(crecv[0], to_x[t]), take(crecv[1], to_x[t])) for t in range(4)]
+    corner_high = [
+        jnp.where(side_lane, take(crecv[2], to_x[t]), take(crecv[3], to_x[t])) for t in range(4)]
     for f in range(5):
         beside = []
         for t in range(4):
-            beside.append(jnp.where(side, take(yrecv[0, f], to_x[t]), take(yrecv[1, f], to_x[t])))
-
-        def row_at(slot, t, f=f):
-            return xrecv[slot, 3 * f + t : 3 * f + t + 1, :]
-
-        def corner(low, high, t, f=f):
-            return jnp.where(side_lane[0:1], row_at(low, t, f), row_at(high, t, f))
+            beside.append(jnp.where(side_lane, take(yrecv[0, f], to_x[t]), take(yrecv[1, f], to_x[t])))
+        rim = [edge_tile(f, t) for t in range(4)]
 
         for s in range(-3, 7):
-            inner = extend(own[f], lambda t: row_at(0, t - 1), lambda t: row_at(3, t), row, s)
+            inner = extend(own[f], lambda t: rim[t], lambda t: rim[t], row, s)
             fields[3, f, s + 3] = inner
             if s < -2 or s > 5:
                 continue
-            outer = extend(beside, lambda t: corner(1, 2, t - 1), lambda t: corner(4, 5, t), row, s)
+            outer = extend(
+                beside, lambda t: corner_low[t][f : f + 1], lambda t: corner_high[t][f : f + 1], row, s)
             for k in (1, 2, 3):
                 if k == 3 and not 0 <= s <= 3:
                     continue
@@ -313,7 +348,6 @@
 
     lax.fori_loop(0, 2, first_sums, 0)
 
-    dam_raw = [dam[:, b, :].astype(jnp.float32) for b in range(BYN)]
     to_raw = [8 * (4 * b + (lane // 4) % 4) + lane // 16 for b in range(BYN)]
     x_in = lane % 4
 
@@ -343,8 +377,7 @@
             trace + 2.0 * SHEAR * strain[n] if n % 4 == 0 else 2.0 * SHEAR * strain[n]
             for n in range(9)
         ]
-        intact = 1.0 - lattice_tile(dam_raw, t)
-        first = [e * intact for e in product(grad, second)]
+        first = [e * own_u[3, t] for e in product(grad, second)]
         mapped = product(first, inv)
         for c in range(3):
             force[c, t] = mapped[3 * c] * span[0] + mapped[3 * c + 1] * span[1] + mapped[3 * c + 2] * span[2]
@@ -362,38 +395,45 @@
         for t in range(1, 4):
             low = jnp.where(block_y == t, lane_roll(of_x[t], 32 * t), low)
             high = jnp.where(block_y == t, lane_roll(of_x[t], 32 * (t - 3)), high)
-        ysend2[0, n] = low
-        ysend2[1, n] = high
+        for k, tile in enumerate((low, high)):
+            ysend2[k, n] = tile
+            for m, r in enumerate((0, 7)):
+                csend2[2 * m + k, n : n + 1, :] = tile[r : r + 1]
         for t in range(4):
             xstress[n, t] = of_x[t]
 
-    copies2 = exchange(xsend2, xrecv2, ysend2, yrecv2, ssem2, rsem2)
+    copies2 = exchange((xsend2, xrecv2), (ysend2, yrecv2), (csend2, crecv2), ssem2, rsem2)
 
     for n in range(9):
         for b in range(BYN):
-            dg_out[b, n] = block_tile([deform[t][n] for t in range(4)], b)
+            dg_out[pl.ds(4 * n + b, 8, stride=36), :] = block_tile([deform[t][n] for t in range(4)], b)
     for copy in copies2:
         copy.wait_recv()
 
+    def corner2(low, high):
+        return [
+            jnp.where(lane[0:1] < 64, lane_roll(crecv2[low], -32 * t), lane_roll(crecv2[high], 32 * (3 - t)))
+            for t in range(4)
+        ]
+
+    corner_low2, corner_high2 = corner2(0, 1), corner2(2, 3)
     for n in range(9):
         mine = [xstress[n, t] for t in range(4)]
         beside = []
         for t in range(4):
             beside.append(jnp.where(
-                side, lane_roll(yrecv2[0, n], -32 * t), lane_roll(yrecv2[1, n], 32 * (3 - t))))
+                side_lane, lane_roll(yrecv2[0, n], -32 * t), lane_roll(yrecv2[1, n], 32 * (3 - t))))
 
         def row_at2(slot, t, n=n):
             return xrecv2[slot, 3 * n + t : 3 * n + t + 1, :]
 
-        def corner2(low, high, t):
-            return jnp.where(side_lane[0:1], row_at2(low, t), row_at2(high, t))
-
         for s in range(-3, 7):
-            inner = extend(mine, lambda t: row_at2(0, t - 1), lambda t: row_at2(3, t), row, s)
+            inner = extend(mine, lambda t: row_at2(0, t - 1), lambda t: row_at2(1, t), row, s)
             ystress[3, n, s + 3] = inner
             if s < -2 or s > 5:
                 continue
-            outer = extend(beside, lambda t: corner2(1, 2, t - 1), lambda t: corner2(4, 5, t), row, s)
+            outer = extend(
+                beside, lambda t: corner_low2[t][n : n + 1], lambda t: corner_high2[t][n : n + 1], row, s)
             for k in (1, 2, 3):
                 if k == 3 and not 0 <= s <= 3:
                     continue
@@ -430,40 +470,63 @@
     lax.fori_loop(0, 3, second_sums, 0)
     for c in range(3):
         for b in range(BYN):
-            force_out[b, c] = block_tile([force[c, t] for t in range(4)], b)
+            force_out[pl.ds(4 * c + b, 8, stride=12), :] = block_tile([force[c, t] for t in range(4)], b)
     for copy in copies + copies2:
         copy.wait_send()
 
 
+def store(dg, force, dg_out, force_out, sem):
+    copies = [
+        pltpu.make_async_copy(dg, dg_out, sem.at[0]),
+        pltpu.make_async_copy(force, force_out, sem.at[1]),
+    ]
+    for copy in copies:
+        copy.start()
+    for copy in copies:
+        copy.wait()
+
+
 def local(displacement, volume, health, damage, block_pairs):
-    pairs = jnp.pad(block_pairs[0, 0].T, ((0, 0), (0, 256 - block_pairs.shape[2])), constant_values=-1)
+    pairs = block_pairs[0, 0].T
+    disp = jnp.transpose(displacement, (0, 2, 1, 3)).reshape(-1, LANES)
+    rows = [a.reshape(-1, LANES) for a in (volume, health, damage)]
     f32 = jnp.float32
     vmem = pl.BlockSpec(memory_space=pltpu.VMEM)
     dg, force = pl.pallas_call(
         kernel,
         out_shape=(
-            jax.ShapeDtypeStruct((BYN, 9, BXN, LANES), f32),
-            jax.ShapeDtypeStruct((BYN, 3, BXN, LANES), f32),
+            pltpu.VMEM((BXN * 9 * BYN, LANES), f32),
+            pltpu.VMEM((BXN * 3 * BYN, LANES), f32),
         ),
-        in_specs=[vmem] * 5,
+        in_specs=[pl.BlockSpec(memory_space=pl.ANY)] * 5,
         out_specs=(vmem, vmem),
         scratch_shapes=[
+            pltpu.VMEM(disp.shape, f32),
+            pltpu.VMEM(rows[0].shape, f32),
+            pltpu.VMEM(rows[1].shape, f32),
+            pltpu.VMEM(rows[2].shape, jnp.int32),
+            pltpu.VMEM(pairs.shape, jnp.int32),
             pltpu.VMEM((2, 6, 8, LANES), f32),
             pltpu.VMEM((2, 6, 8, LANES), f32),
-            pltpu.VMEM((2, 16, LANES), f32),
-            pltpu.VMEM((6, 16, LANES), f32),
+            pltpu.VMEM((2, 24, LANES), f32),
+            pltpu.VMEM((2, 24, LANES), f32),
+            pltpu.VMEM((4, 8, LANES), f32),
+            pltpu.VMEM((4, 8, LANES), f32),
             pltpu.VMEM((2, 9, 8, LANES), f32),
             pltpu.VMEM((2, 9, 8, LANES), f32),
             pltpu.VMEM((2, 32, LANES), f32),
-            pltpu.VMEM((6, 32, LANES), f32),
+            pltpu.VMEM((2, 32, LANES), f32),
+            pltpu.VMEM((4, 16, LANES), f32),
+            pltpu.VMEM((4, 16, LANES), f32),
             pltpu.VMEM((7, 5, 10, 8, LANES), f32),
-            pltpu.VMEM((3, 4, 8, LANES), f32),
+            pltpu.VMEM((4, 4, 8, LANES), f32),
             pltpu.VMEM((7, 7, 4, 8, LANES), f32),
             pltpu.VMEM((W_COUNT, 4, 8, LANES), f32),
             pltpu.VMEM((18, 4, 8, LANES), f32),
             pltpu.VMEM((7, 9, 10, 8, LANES), f32),
             pltpu.VMEM((9, 4, 8, LANES), f32),
             pltpu.VMEM((3, 4, 8, LANES), f32),
+            pltpu.SemaphoreType.DMA((5,)),
             pltpu.SemaphoreType.DMA((8,)),
             pltpu.SemaphoreType.DMA((8,)),
             pltpu.SemaphoreType.DMA((8,)),
@@ -471,8 +534,22 @@
         ],
         compiler_params=pltpu.CompilerParams(collective_id=0, has_side_effects=True),
         name="peridynamics",
-    )(displacement, volume, health, damage, pairs)
-    return jnp.transpose(dg, (2, 0, 1, 3)), jnp.transpose(force, (2, 0, 1, 3))
+    )(disp, *rows, pairs)
+    dg, force = (pltpu.with_memory_space_constraint(a, pltpu.VMEM) for a in (dg, force))
+    hbm = pl.BlockSpec(memory_space=pltpu.HBM)
+    dg, force = pl.pallas_call(
+        store,
+        out_shape=(
+            jax.ShapeDtypeStruct(dg.shape, f32),
+            jax.ShapeDtypeStruct(force.shape, f32),
+        ),
+        in_specs=[vmem] * 2,
+        out_specs=(hbm, hbm),
+        scratch_shapes=[pltpu.SemaphoreType.DMA((2,))],
+        name="store",
+    )(dg, force)
+    dg, force = (a.reshape(BXN, -1, BYN, LANES) for a in (dg, force))
+    return jnp.transpose(dg, (0, 2, 1, 3)), jnp.transpose(force, (0, 2, 1, 3))
 
 
 def solution(mesh):

time: 40.2 us -> 34.4 us (0.86)
  local copies, waits for them, and re-layouts: 4.99 us -> 0 us
  Pallas kernels: 34.3 us -> 33.5 us
    unnamed x5 -> x0, local copies, waits for them, and re-layouts: 3.7 us -> none
    pad x1 -> x0, local copies, waits for them, and re-layouts: 1.29 us -> none  [local(): jnp.pad(block_pairs[0, 0].T, ((0, 0), (0, 256 - block_pairs.shape[2])), c...]
    pallas_call x1 -> x2, Pallas kernels: 34.3 us -> 33.5 us  [the longest x1 32.8 us: local(): pl.pallas_call(kernel, out_shape=(pltpu.VMEM((BXN * 9 * BYN, LANES), f32)...]
where the time goes in v2:
time: 34.4 us; the launch traced here: 34.2 us
  Pallas kernels  33.5 us (97%)
  between operations  0.64 us (2%)
    pallas_call x1, Pallas kernels, local(): pl.pallas_call(kernel, out_shape=(pltpu.VMEM((BXN * 9 * BYN, LANES), f32)...  32.8 us
    pallas_call x1, Pallas kernels, local(): pl.pallas_call(store, out_shape=(jax.ShapeDtypeStruct(dg.shape, f32), jax...  0.69 us

profile of v2, /device:TPU:25, one launch (start us, length us, event | category | flops | bytes accessed | tf_op | source)
XLA Modules:
  0.0 34.2 jit_solution(17632250346427681148)
XLA Ops:
  0.6 32.8 %peridynamics.1 = (f32[288,128]{1,0:T(8,128)S(1)}, f32[96,128]{1,0:T(8,128)S(1)}) custom-call(f32[96,128]{1,0:T(8,128)} %bitcast.15, f32[32,128]{1,0:T(8,128)} %bitcast.16, f32[32,128]{1,0:T(8,128)} %bitcast.17, s32[32,128]{1,0:T(8,128)} %bitcast.18, s32[4,162]{1,0:T(4,128)} %bitcast.19), custom_call_target="tpu_custom_call" | custom-call | tf_op jit(solution)/shard_map/peridynamics/pallas_call | solution.py:495
  33.5 0.7 %store.1 = (f32[288,128]{1,0:T(8,128)}, f32[96,128]{1,0:T(8,128)}) custom-call(f32[288,128]{1,0:T(8,128)S(1)} %get-tuple-element.6.dg, f32[96,128]{1,0:T(8,128)S(1)} %get-tuple-element.7.force), custom_call_target="tpu_custom_call" | custom-call | tf_op jit(solution)/shard_map/store/pallas_call | solution.py:540

commit v3 on v2

--- a/solution.py
+++ b/solution.py
@@ -23,6 +23,12 @@
 CORNERS = ((-1, 1), (-1, -1), (1, 1), (1, -1))
 
 
+REACH_TWO = {0: (2, 0, -2), 1: (3, 1, -2), 2: (3, 0, -1), 4: (1, 3, 2), 5: (0, 2, 2), 6: (0, 3, 1)}
+REACH_THREE = {0: (1, 0, -3), 1: (2, 1, -3), 2: (3, 2, -3), 4: (2, 3, 3), 5: (1, 2, 3), 6: (0, 1, 3)}
+ORDER = ["xx", "xy", "xz", "yy", "yz", "zz"] + [(a, k) for k in range(4) for a in "xyz"]
+ENDS = [key for key in COLUMNS if COLUMNS[key] >= 1]
+
+
 def direction(cx, cy):
     q = 3 * cx + cy
     return q - 1 if q > 0 else 3 - q
@@ -75,12 +81,32 @@
     return value if total is None else total + value
 
 
-def extend(own, low_row, high_row, row, s):
+def extend(own, row, s):
     if s < 0:
-        return jnp.where(row == 0, low_row(s + 4), row_roll(own[s + 4], 1))
+        return jnp.where(row == 0, 0.0, row_roll(own[s + 4], 1))
     if s > 3:
-        return jnp.where(row == 7, high_row(s - 4), row_roll(own[s - 4], -1))
+        return jnp.where(row == 7, 0.0, row_roll(own[s - 4], -1))
     return own[s]
+
+
+def place(row, table, tile_of):
+    got = jnp.zeros((8, LANES), jnp.float32)
+    for r, (tile, _, _) in table.items():
+        got = jnp.where(row == r, tile_of(r < 4, tile), got)
+    return got
+
+
+def ends_of(row, packed, three):
+    gone = jnp.where(row % 4 == 2, 0.0, packed)
+    return gone + jnp.where(row % 4 == 0, row_roll(packed, -2), 0.0) + three
+
+
+def with_ends(tile, ends, row, t):
+    if t <= 2:
+        tile = tile + jnp.where(row == 0, ends[t : t + 1], 0.0)
+    if t >= 1:
+        tile = tile + jnp.where(row == 7, ends[7 - t : 8 - t], 0.0)
+    return tile
 
 
 def kernel(
@@ -88,7 +114,7 @@
     disp, vol, hea, dam, pairs,
     ysend, yrecv, xsend, xrecv, csend, crecv,
     ysend2, yrecv2, xsend2, xrecv2, csend2, crecv2,
-    fields, own_u, health_m, weights, sums, ystress, xstress, force,
+    fields, own_u, health_m, weights, sums, ystress, xstress, force, end_weights,
     isem, ssem, rsem, ssem2, rsem2,
 ):
     loads = [
@@ -188,24 +214,18 @@
         for c in range(3):
             own_u[c, t] = lattice_tile([u_tile(c, b) for b in range(BYN)], t)
         own_u[3, t] = 1.0 - lattice_tile(dam_raw, t)
-    for copy in copies:
+    for copy in copies[2:4]:
         copy.wait_recv()
 
-    def flag_ext(tile, low, high, cx):
+    def flag_ext(tile, cx):
         if cx == 0:
             return tile
-        if cx < 0:
-            return jnp.where(row == 0, low, row_roll(tile, 1))
-        return jnp.where(row == 7, high, row_roll(tile, -1))
+        return jnp.where(row == (0 if cx < 0 else 7), 0.0, row_roll(tile, -cx))
 
     seen = {}
-    for cy, tile, low, high in (
-        (0, flags, xrecv[0, 20:21, :], xrecv[1, 20:21, :]),
-        (1, yrecv[0, 5], crecv[0, 5:6, :], crecv[2, 5:6, :]),
-        (-1, yrecv[1, 5], crecv[1, 5:6, :], crecv[3, 5:6, :]),
-    ):
+    for cy, tile in ((0, flags), (1, yrecv[0, 5]), (-1, yrecv[1, 5])):
         for cx in (-1, 0, 1):
-            seen[(cx, cy)] = flag_ext(tile, low, high, cx)
+            seen[(cx, cy)] = flag_ext(tile, cx)
     enabled = {}
     for cx in (-1, 0, 1):
         for cy in (-1, 0, 1):
@@ -242,34 +262,16 @@
                 health_m[dy + 3, dx + 3, t] = h if by_cx[cx] is None else h * by_cx[cx]
 
     side_lane = lane < 64
-    edge = [
-        jnp.concatenate([xrecv[0, 4 * k : 4 * k + 4, :], xrecv[1, 4 * k : 4 * k + 4, :]], axis=0)
-        for k in (4, 3, 0, 1, 2)
-    ]
-    edge = edge[:2] + [edge[1] * e for e in edge[2:]]
-
-    def edge_tile(f, t):
-        got = jnp.where(row % 4 == block_y, take(edge[f], to_x[t]), 0.0)
-        got = got + jnp.where(row % 2 == 0, row_roll(got, -1), row_roll(got, 1))
-        return got + jnp.where(row % 4 < 2, row_roll(got, -2), row_roll(got, 2))
-
-    corner_low = [
-        jnp.where(side_lane, take(crecv[0], to_x[t]), take(crecv[1], to_x[t])) for t in range(4)]
-    corner_high = [
-        jnp.where(side_lane, take(crecv[2], to_x[t]), take(crecv[3], to_x[t])) for t in range(4)]
     for f in range(5):
         beside = []
         for t in range(4):
             beside.append(jnp.where(side_lane, take(yrecv[0, f], to_x[t]), take(yrecv[1, f], to_x[t])))
-        rim = [edge_tile(f, t) for t in range(4)]
-
         for s in range(-3, 7):
-            inner = extend(own[f], lambda t: rim[t], lambda t: rim[t], row, s)
+            inner = extend(own[f], row, s)
             fields[3, f, s + 3] = inner
             if s < -2 or s > 5:
                 continue
-            outer = extend(
-                beside, lambda t: corner_low[t][f : f + 1], lambda t: corner_high[t][f : f + 1], row, s)
+            outer = extend(beside, row, s)
             for k in (1, 2, 3):
                 if k == 3 and not 0 <= s <= 3:
                     continue
@@ -341,12 +343,128 @@
             for name in ("xx", "zz", "xz"):
                 if name in part:
                     total[name] = add(total.get(name), part[name])
-        order = ["xx", "xy", "xz", "yy", "yz", "zz"] + [(a, k) for k in range(4) for a in "xyz"]
-        for n, name in enumerate(order):
+        for n, name in enumerate(ORDER):
             sums[n, pl.ds(base, 2)] = total[name]
         return carry
 
     lax.fori_loop(0, 2, first_sums, 0)
+
+    for copy in copies[:2] + copies[4:]:
+        copy.wait_recv()
+    edge = [
+        jnp.concatenate([xrecv[0, 4 * k : 4 * k + 4, :], xrecv[1, 4 * k : 4 * k + 4, :]], axis=0)
+        for k in (4, 3, 0, 1, 2)
+    ]
+    edge = edge[:2] + [edge[1] * e for e in edge[2:]]
+
+    def edge_tile(f, t):
+        got = jnp.where(row % 4 == block_y, take(edge[f], to_x[t]), 0.0)
+        got = got + jnp.where(row % 2 == 0, row_roll(got, -1), row_roll(got, 1))
+        return got + jnp.where(row % 4 < 2, row_roll(got, -2), row_roll(got, 2))
+
+    corner_low = [
+        jnp.where(side_lane, take(crecv[0], to_x[t]), take(crecv[1], to_x[t])) for t in range(4)]
+    corner_high = [
+        jnp.where(side_lane, take(crecv[2], to_x[t]), take(crecv[3], to_x[t])) for t in range(4)]
+
+    low_end = row < 4
+
+    def end_rows(low, high):
+        return jnp.where(low_end, low, high)
+
+    end_flags = end_rows(flags[0:1], flags[7:8])
+    end_seen = {
+        0: end_rows(xrecv[0, 20:21, :], xrecv[1, 20:21, :]),
+        1: end_rows(crecv[0, 5:6, :], crecv[2, 5:6, :]),
+        -1: end_rows(crecv[1, 5:6, :], crecv[3, 5:6, :]),
+    }
+    end_enabled = {}
+    for cy in (-1, 0, 1):
+        forth = jnp.where(low_end, direction(-1, cy), direction(1, cy))
+        back = jnp.where(low_end, direction(1, -cy), direction(-1, -cy))
+        theirs = take(end_seen[0], 8 * (block_y + cy + 1) + back)
+        if cy == 1:
+            theirs = jnp.where(block_y == 3, take(end_seen[1], 8 + back), theirs)
+        if cy == -1:
+            theirs = jnp.where(block_y == 0, take(end_seen[-1], 32 + back), theirs)
+        mine = take(end_flags, 8 * (block_y + 1) + forth)
+        end_enabled[cy] = jnp.minimum(jnp.maximum(mine, theirs), 1.0)
+
+    def end_health(table):
+        got = jnp.zeros((8, LANES), jnp.float32)
+        for r, (_, t, _) in table.items():
+            got = jnp.where(row == r, own[0][t][0:1] if r < 4 else own[0][t][7:8], got)
+        return got
+
+    def steps(table):
+        got = jnp.zeros((8, LANES), jnp.float32)
+        for r, (_, _, dx) in table.items():
+            got = jnp.where(row == r, float(dx), got)
+        return got
+
+    step_two, step_three = steps(REACH_TWO), steps(REACH_THREE)
+    health_two = end_health(REACH_TWO)
+    end_fields = {0: [], 1: [], 3: []}
+    for f in range(5):
+        rim = [edge_tile(f, t) for t in range(4)]
+        end_fields[0].append(place(row, REACH_TWO, lambda low, t: rim[t]))
+        end_fields[1].append(place(
+            row, REACH_TWO, lambda low, t: (corner_low if low else corner_high)[t][f : f + 1]))
+        end_fields[3].append(place(row, REACH_THREE, lambda low, t: rim[t]))
+
+    end_total = {}
+    for dy in range(-2, 3):
+        held = health_two
+        if dy > 0:
+            held = health_two * jnp.where(y_in + dy >= 4, end_enabled[1], end_enabled[0])
+        elif dy < 0:
+            held = health_two * jnp.where(y_in + dy < 0, end_enabled[-1], end_enabled[0])
+        else:
+            held = health_two * end_enabled[0]
+        src_y = []
+        for f in range(5):
+            inner, outer = end_fields[0][f], end_fields[1][f]
+            if dy > 0:
+                inner = jnp.where(y_at < dy, outer, inner)
+            elif dy < 0:
+                inner = jnp.where(y_at >= 16 + dy, outer, inner)
+            src_y.append(inner)
+        part = {}
+        for dz in range(-3, 4):
+            if COLUMNS.get((dy, dz), 0) < 1:
+                continue
+            src = [lane_roll(e, -(8 * dy + dz)) for e in src_y]
+            h = src[0]
+            if dz != 0:
+                h = jnp.where(z_ok[dz], h, 0.0)
+            if COLUMNS[(dy, dz)] == 1:
+                h = jnp.where(row % 4 == 2, h, 0.0)
+            w = jnp.minimum(held, h)
+            end_weights[ENDS.index((dy, dz))] = w
+            for k in range(4):
+                value = w * src[k + 1]
+                part["s", k] = add(part.get(("s", k)), value)
+                if dz != 0:
+                    part["z", k] = add(part.get(("z", k)), times(dz, value))
+                    if k == 0:
+                        part["zz"] = add(part.get("zz"), times(dz * dz, value))
+        for name in part:
+            end_total[name] = add(end_total.get(name), part[name])
+        if dy != 0:
+            for k in range(4):
+                end_total["y", k] = add(end_total.get(("y", k)), times(dy, part["s", k]))
+            end_total["yy"] = add(end_total.get("yy"), times(dy * dy, part["s", 0]))
+            end_total["yz"] = add(end_total.get("yz"), times(dy, part["z", 0]))
+    for k in range(4):
+        end_total["x", k] = step_two * end_total["s", k]
+    end_total["xx"] = step_two * end_total["x", 0]
+    end_total["xy"] = step_two * end_total["y", 0]
+    end_total["xz"] = step_two * end_total["z", 0]
+    w = jnp.minimum(end_health(REACH_THREE) * end_enabled[0], end_fields[3][0])
+    end_weights[len(ENDS)] = w
+    three = {("x", k): step_three * (w * end_fields[3][k + 1]) for k in range(4)}
+    three["xx"] = step_three * three["x", 0]
+    end_sums = [ends_of(row, end_total[name], three.get(name, 0.0)) for name in ORDER]
 
     to_raw = [8 * (4 * b + (lane // 4) % 4) + lane // 16 for b in range(BYN)]
     x_in = lane % 4
@@ -359,11 +477,12 @@
 
     deform, stress = [], []
     for t in range(4):
-        kxx, kxy, kxz, kyy, kyz, kzz = (sums[n, t] for n in range(6))
-        span = [sums[6 + n, t] for n in range(3)]
+        full = [with_ends(sums[n, t], end_sums[n], row, t) for n in range(18)]
+        kxx, kxy, kxz, kyy, kyz, kzz = full[:6]
+        span = full[6:9]
         sym = [kxx, kxy, kxz, kxy, kyy, kyz, kxz, kyz, kzz]
         moment = [
-            sym[3 * c + d] + sums[9 + 3 * c + d, t] - own_u[c, t] * span[d]
+            sym[3 * c + d] + full[9 + 3 * c + d] - own_u[c, t] * span[d]
             for c in range(3) for d in range(3)
         ]
         shape = [sym[n] + 1.0 if n % 4 == 0 else sym[n] for n in range(9)]
@@ -407,16 +526,9 @@
     for n in range(9):
         for b in range(BYN):
             dg_out[pl.ds(4 * n + b, 8, stride=36), :] = block_tile([deform[t][n] for t in range(4)], b)
-    for copy in copies2:
+    for copy in copies2[2:4]:
         copy.wait_recv()
 
-    def corner2(low, high):
-        return [
-            jnp.where(lane[0:1] < 64, lane_roll(crecv2[low], -32 * t), lane_roll(crecv2[high], 32 * (3 - t)))
-            for t in range(4)
-        ]
-
-    corner_low2, corner_high2 = corner2(0, 1), corner2(2, 3)
     for n in range(9):
         mine = [xstress[n, t] for t in range(4)]
         beside = []
@@ -424,16 +536,12 @@
             beside.append(jnp.where(
                 side_lane, lane_roll(yrecv2[0, n], -32 * t), lane_roll(yrecv2[1, n], 32 * (3 - t))))
 
-        def row_at2(slot, t, n=n):
-            return xrecv2[slot, 3 * n + t : 3 * n + t + 1, :]
-
         for s in range(-3, 7):
-            inner = extend(mine, lambda t: row_at2(0, t - 1), lambda t: row_at2(1, t), row, s)
+            inner = extend(mine, row, s)
             ystress[3, n, s + 3] = inner
             if s < -2 or s > 5:
                 continue
-            outer = extend(
-                beside, lambda t: corner_low2[t][n : n + 1], lambda t: corner_high2[t][n : n + 1], row, s)
+            outer = extend(beside, row, s)
             for k in (1, 2, 3):
                 if k == 3 and not 0 <= s <= 3:
                     continue
@@ -468,9 +576,51 @@
         return carry
 
     lax.fori_loop(0, 3, second_sums, 0)
+
+    for copy in copies2[:2] + copies2[4:]:
+        copy.wait_recv()
+
+    def corner2(low, high):
+        return [
+            jnp.where(lane[0:1] < 64, lane_roll(crecv2[low], -32 * t), lane_roll(crecv2[high], 32 * (3 - t)))
+            for t in range(4)
+        ]
+
+    corner_low2, corner_high2 = corner2(0, 1), corner2(2, 3)
+
+    def halo_row(n, low, t):
+        return xrecv2[0, 3 * n + t - 1 : 3 * n + t, :] if low else xrecv2[1, 3 * n + t : 3 * n + t + 1, :]
+
+    end_inner, end_outer, end_force = [], [], []
+    for n in range(9):
+        scale = step_two if n % 3 == 0 else 1.0
+        end_inner.append(scale * place(row, REACH_TWO, lambda low, t: halo_row(n, low, t)))
+        end_outer.append(scale * place(
+            row, REACH_TWO, lambda low, t: (corner_low2 if low else corner_high2)[t][n : n + 1]))
     for c in range(3):
+        total = None
+        for dy in range(-2, 3):
+            src_y = []
+            for d in range(3):
+                inner, outer = end_inner[3 * c + d], end_outer[3 * c + d]
+                if dy > 0:
+                    inner = jnp.where(y_at < dy, outer, inner)
+                elif dy < 0:
+                    inner = jnp.where(y_at >= 16 + dy, outer, inner)
+                src_y.append(inner)
+            fixed = src_y[0] if dy == 0 else src_y[0] + times(dy, src_y[1])
+            for dz in range(-3, 4):
+                if COLUMNS.get((dy, dz), 0) < 1:
+                    continue
+                value = fixed if dz == 0 else fixed + times(dz, src_y[2])
+                value = lane_roll(value, -(8 * dy + dz))
+                total = add(total, end_weights[ENDS.index((dy, dz))] * value)
+        three = step_three * place(row, REACH_THREE, lambda low, t: halo_row(3 * c, low, t))
+        end_force.append(ends_of(row, total, end_weights[len(ENDS)] * three))
+    for c in range(3):
+        full_force = [with_ends(force[c, t], end_force[c], row, t) for t in range(4)]
         for b in range(BYN):
-            force_out[pl.ds(4 * c + b, 8, stride=12), :] = block_tile([force[c, t] for t in range(4)], b)
+            force_out[pl.ds(4 * c + b, 8, stride=12), :] = block_tile(full_force, b)
     for copy in copies + copies2:
         copy.wait_send()
 
@@ -526,6 +676,7 @@
             pltpu.VMEM((7, 9, 10, 8, LANES), f32),
             pltpu.VMEM((9, 4, 8, LANES), f32),
             pltpu.VMEM((3, 4, 8, LANES), f32),
+            pltpu.VMEM((len(ENDS) + 1, 8, LANES), f32),
             pltpu.SemaphoreType.DMA((5,)),
             pltpu.SemaphoreType.DMA((8,)),
             pltpu.SemaphoreType.DMA((8,)),

time: 34.4 us -> 31.2 us (0.907)
  Pallas kernels: 33.5 us -> 30.4 us
    pallas_call x1, Pallas kernels: 32.8 us -> 29.7 us  [local(): pl.pallas_call(kernel, out_shape=(pltpu.VMEM((BXN * 9 * BYN, LANES), f32)...]
where the time goes in v3:
time: 31.2 us; the launch traced here: 31 us
  Pallas kernels  30.4 us (97%)
  between operations  0.64 us (2%)
    pallas_call x1, Pallas kernels, local(): pl.pallas_call(kernel, out_shape=(pltpu.VMEM((BXN * 9 * BYN, LANES), f32)...  29.7 us
    pallas_call x1, Pallas kernels, local(): pl.pallas_call(store, out_shape=(jax.ShapeDtypeStruct(dg.shape, f32), jax...  0.69 us

profile of v3, /device:TPU:25, one launch (start us, length us, event | category | flops | bytes accessed | tf_op | source)
XLA Modules:
  0.0 31.0 jit_solution(16289741239273770323)
XLA Ops:
  0.6 29.7 %peridynamics.1 = (f32[288,128]{1,0:T(8,128)S(1)}, f32[96,128]{1,0:T(8,128)S(1)}) custom-call(f32[96,128]{1,0:T(8,128)} %bitcast.15, f32[32,128]{1,0:T(8,128)} %bitcast.16, f32[32,128]{1,0:T(8,128)} %bitcast.17, s32[32,128]{1,0:T(8,128)} %bitcast.18, s32[4,162]{1,0:T(4,128)} %bitcast.19), custom_call_target="tpu_custom_call" | custom-call | tf_op jit(solution)/shard_map/peridynamics/pallas_call | solution.py:645
  30.4 0.7 %store.1 = (f32[288,128]{1,0:T(8,128)}, f32[96,128]{1,0:T(8,128)}) custom-call(f32[288,128]{1,0:T(8,128)S(1)} %get-tuple-element.6.dg, f32[96,128]{1,0:T(8,128)S(1)} %get-tuple-element.7.force), custom_call_target="tpu_custom_call" | custom-call | tf_op jit(solution)/shard_map/store/pallas_call | solution.py:691

commit v4 on v3

--- a/solution.py
+++ b/solution.py
@@ -26,6 +26,8 @@
 REACH_TWO = {0: (2, 0, -2), 1: (3, 1, -2), 2: (3, 0, -1), 4: (1, 3, 2), 5: (0, 2, 2), 6: (0, 3, 1)}
 REACH_THREE = {0: (1, 0, -3), 1: (2, 1, -3), 2: (3, 2, -3), 4: (2, 3, 3), 5: (1, 2, 3), 6: (0, 1, 3)}
 ORDER = ["xx", "xy", "xz", "yy", "yz", "zz"] + [(a, k) for k in range(4) for a in "xyz"]
+OTHERS = (-3, -2, -1, 1, 2, 3)
+FIRST = 0
 ENDS = [key for key in COLUMNS if COLUMNS[key] >= 1]
 
 
@@ -81,12 +83,15 @@
     return value if total is None else total + value
 
 
-def extend(own, row, s):
-    if s < 0:
-        return jnp.where(row == 0, 0.0, row_roll(own[s + 4], 1))
-    if s > 3:
-        return jnp.where(row == 7, 0.0, row_roll(own[s - 4], -1))
-    return own[s]
+def spread(own, deep, clear=None):
+    if deep == 0:
+        return own
+    low = pltpu.roll(own[4 - deep :], 1, axis=1)
+    high = pltpu.roll(own[:deep], 7, axis=1)
+    if clear is not None:
+        low = jnp.where(clear == 0, 0.0, low)
+        high = jnp.where(clear == 7, 0.0, high)
+    return jnp.concatenate([low, own, high], axis=0)
 
 
 def place(row, table, tile_of):
@@ -114,7 +119,7 @@
     disp, vol, hea, dam, pairs,
     ysend, yrecv, xsend, xrecv, csend, crecv,
     ysend2, yrecv2, xsend2, xrecv2, csend2, crecv2,
-    fields, own_u, health_m, weights, sums, ystress, xstress, force, end_weights,
+    fields, own_u, health_m, weights, sums, ystress, force, end_weights,
     isem, ssem, rsem, ssem2, rsem2,
 ):
     loads = [
@@ -128,13 +133,47 @@
     me_x, me_y = lax.axis_index("gx"), lax.axis_index("gy")
 
     def device(cx, cy):
-        return (lax.rem(me_x + (cx + n_gx), n_gx), lax.rem(me_y + (cy + n_gy), n_gy))
+        return (me_x + cx, me_y + cy)
+
+    inside = {-1: (me_x > 0, me_y > 0), 1: (me_x < n_gx - 1, me_y < n_gy - 1)}
+
+    def present(cx, cy):
+        if cx and cy:
+            return jnp.logical_and(inside[cx][0], inside[cy][1])
+        return inside[cx][0] if cx else inside[cy][1]
 
     barrier = pltpu.get_barrier_semaphore()
     for cx in (-1, 0, 1):
         for cy in (-1, 0, 1):
             if cx or cy:
-                pl.semaphore_signal(barrier, inc=1, device_id=device(cx, cy), device_id_type=MESH)
+
+                @pl.when(present(cx, cy))
+                def _():
+                    pl.semaphore_signal(
+                        barrier, inc=1, device_id=device(cx, cy), device_id_type=MESH)
+
+    spans = [
+        1 + inside[-1][axis].astype(jnp.int32) + inside[1][axis].astype(jnp.int32) for axis in (0, 1)]
+    for n, cx in enumerate((-1, 1)):
+
+        @pl.when(jnp.logical_not(present(cx, 0)))
+        def _():
+            xrecv[n] = jnp.zeros(xrecv.shape[1:], jnp.float32)
+            xrecv2[n] = jnp.zeros(xrecv2.shape[1:], jnp.float32)
+
+    for n, cy in enumerate((1, -1)):
+
+        @pl.when(jnp.logical_not(present(0, cy)))
+        def _():
+            yrecv[n] = jnp.zeros(yrecv.shape[1:], jnp.float32)
+            yrecv2[n] = jnp.zeros(yrecv2.shape[1:], jnp.float32)
+
+    for n, (cx, cy) in enumerate(CORNERS):
+
+        @pl.when(jnp.logical_not(present(cx, cy)))
+        def _():
+            crecv[n] = jnp.zeros(crecv.shape[1:], jnp.float32)
+            crecv2[n] = jnp.zeros(crecv2.shape[1:], jnp.float32)
 
     row, lane = iota(0), iota(1)
     block_y, y_in, z_at = lane // 32, (lane // 8) % 4, lane % 8
@@ -177,7 +216,7 @@
         xsend[m, 12:16, :] = vol[4 * r : 4 * r + 4, :]
         xsend[m, 16:20, :] = hea[4 * r : 4 * r + 4, :]
         xsend[m, 20:21, :] = flags[r : r + 1]
-    pl.semaphore_wait(barrier, 8)
+    pl.semaphore_wait(barrier, spans[0] * spans[1] - 1)
 
     def exchange(x_pair, y_pair, c_pair, sends, recvs):
         moves = []
@@ -189,14 +228,25 @@
             at = 2 * (0 if cx == 1 else 1) + (0 if cy == 1 else 1)
             moves.append((c_pair[0].at[at], c_pair[1].at[n], -cx, -cy))
         copies = [
-            pltpu.make_async_remote_copy(
+            (pltpu.make_async_remote_copy(
                 src_ref=src, dst_ref=dst, send_sem=sends.at[n], recv_sem=recvs.at[n],
-                device_id=device(tx, ty), device_id_type=MESH)
+                device_id=device(tx, ty), device_id_type=MESH), tx, ty)
             for n, (src, dst, tx, ty) in enumerate(moves)
         ]
-        for copy in copies:
-            copy.start()
+        for copy, tx, ty in copies:
+
+            @pl.when(present(tx, ty))
+            def _():
+                copy.start()
+
         return copies
+
+    def arrive(copies):
+        for copy, tx, ty in copies:
+
+            @pl.when(present(-tx, -ty))
+            def _():
+                copy.wait_recv()
 
     copies = exchange((xsend, xrecv), (ysend, yrecv), (csend, crecv), ssem, rsem)
 
@@ -214,21 +264,17 @@
         for c in range(3):
             own_u[c, t] = lattice_tile([u_tile(c, b) for b in range(BYN)], t)
         own_u[3, t] = 1.0 - lattice_tile(dam_raw, t)
-    for copy in copies[2:4]:
-        copy.wait_recv()
-
     def flag_ext(tile, cx):
         if cx == 0:
             return tile
         return jnp.where(row == (0 if cx < 0 else 7), 0.0, row_roll(tile, -cx))
 
-    seen = {}
-    for cy, tile in ((0, flags), (1, yrecv[0, 5]), (-1, yrecv[1, 5])):
+    seen, enabled = {}, {}
+
+    def see(cy, tile):
         for cx in (-1, 0, 1):
             seen[(cx, cy)] = flag_ext(tile, cx)
-    enabled = {}
-    for cx in (-1, 0, 1):
-        for cy in (-1, 0, 1):
+        for cx in (-1, 0, 1):
             if cx == 0 and cy == 0:
                 continue
             mine = take(flags, 8 * (block_y + 1) + direction(cx, cy))
@@ -240,117 +286,127 @@
                 theirs = jnp.where(block_y == 0, take(seen[(cx, -1)], 32 + back + 0 * lane), theirs)
             enabled[(cx, cy)] = jnp.minimum(jnp.maximum(mine, theirs), 1.0)
 
-    for dy in range(-3, 4):
-        deep = max(m for (a, _), m in COLUMNS.items() if a == dy)
-        by_cx = {}
-        for cx in (-1, 0, 1):
-            near = enabled.get((cx, 0))
-            if dy > 0:
-                far = enabled[(cx, 1)]
+    def hold_health(dys):
+        for dy in dys:
+            deep = max(m for (a, _), m in COLUMNS.items() if a == dy)
+            by_cx = {}
+            for cx in (-1, 0, 1):
+                near = enabled.get((cx, 0))
+                if dy == 0:
+                    by_cx[cx] = near
+                    continue
                 near = 1.0 if near is None else near
-                by_cx[cx] = jnp.where(y_in + dy >= 4, far, near)
-            elif dy < 0:
-                far = enabled[(cx, -1)]
-                near = 1.0 if near is None else near
-                by_cx[cx] = jnp.where(y_in + dy < 0, far, near)
-            else:
-                by_cx[cx] = near
-        for dx in range(-deep, deep + 1):
-            for t in range(4):
-                cx = (t + dx) // 4
-                h = own[0][t]
-                health_m[dy + 3, dx + 3, t] = h if by_cx[cx] is None else h * by_cx[cx]
-
-    side_lane = lane < 64
-    for f in range(5):
-        beside = []
-        for t in range(4):
-            beside.append(jnp.where(side_lane, take(yrecv[0, f], to_x[t]), take(yrecv[1, f], to_x[t])))
-        for s in range(-3, 7):
-            inner = extend(own[f], row, s)
-            fields[3, f, s + 3] = inner
-            if s < -2 or s > 5:
-                continue
-            outer = extend(beside, row, s)
-            for k in (1, 2, 3):
-                if k == 3 and not 0 <= s <= 3:
-                    continue
-                fields[3 + k, f, s + 3] = jnp.where(y_at < k, outer, inner)
-                fields[3 - k, f, s + 3] = jnp.where(y_at >= 16 - k, outer, inner)
+                if dy > 0:
+                    by_cx[cx] = jnp.where(y_in + dy >= 4, enabled[(cx, 1)], near)
+                else:
+                    by_cx[cx] = jnp.where(y_in + dy < 0, enabled[(cx, -1)], near)
+            for dx in range(-deep, deep + 1):
+                for t in range(4):
+                    flag = by_cx[(t + dx) // 4]
+                    h = own[0][t]
+                    health_m[dy + 3, dx + 3, t] = h if flag is None else h * flag
 
     z_ok = {dz: (z_at + dz >= 0) & (z_at + dz < 8) for dz in range(-3, 4)}
 
-    def first_sums(half, carry):
-        base = 2 * half
+    def dz_of(dy):
+        return [dz for dz in range(-3, 4) if (dy, dz) in COLUMNS]
+
+    def gather_sums(k, dys, fresh):
         total = {}
-        for dy in range(-3, 4):
+        for dy in dys:
             part = {}
-            for dz in range(-3, 4):
-                if (dy, dz) not in COLUMNS:
-                    continue
+            for dz in dz_of(dy):
                 deep = COLUMNS[(dy, dz)]
                 turn = -(8 * dy + dz)
-                src = [
-                    lane_roll(fields[dy + 3, f, pl.ds(base + 3 - deep, 2 + 2 * deep)], turn)
-                    for f in range(5)
-                ]
-                if dz != 0:
-                    src[0] = jnp.where(z_ok[dz][None], src[0], 0.0)
-                a0, a1, a2 = [None] * 4, [None] * 4, None
+                value = spread(lane_roll(fields[dy + 3, k + 1], turn), deep)
+                if k is FIRST:
+                    h = lane_roll(fields[dy + 3, 0], turn)
+                    if dz != 0:
+                        h = jnp.where(z_ok[dz][None], h, 0.0)
+                    h = spread(h, deep, row[None])
+                a0, a1, a2 = None, None, None
                 for reach in range(deep + 1):
                     terms = []
                     for dx in (reach, -reach) if reach else (0,):
                         lo = deep + dx
-                        w = jnp.minimum(
-                            health_m[dy + 3, dx + 3, pl.ds(base, 2)], src[0][lo : lo + 2])
-                        weights[W_AT[(dy, dz)] + lo, pl.ds(base, 2)] = w
+                        at = W_AT[(dy, dz)] + lo
                         if dy == 0 and dz == 0 and dx == 0:
                             continue
-                        terms.append([w * src[k + 1][lo : lo + 2] for k in range(4)])
+                        if k is FIRST:
+                            w = jnp.minimum(health_m[dy + 3, dx + 3], h[lo : lo + 4])
+                            weights[at] = w
+                        else:
+                            w = weights[at]
+                        terms.append(w * value[lo : lo + 4])
                     if not terms:
                         continue
-                    for k in range(4):
-                        both = terms[0][k] if reach == 0 else terms[0][k] + terms[1][k]
-                        a0[k] = add(a0[k], both)
-                        if reach:
-                            a1[k] = add(a1[k], times(reach, terms[0][k] - terms[1][k]))
-                            if k == 0:
-                                a2 = add(a2, times(reach * reach, both))
-                for k in range(4):
-                    if dy != 0:
-                        part["y", k] = add(part.get(("y", k)), a0[k])
-                    if dz != 0:
-                        part["z", k] = add(part.get(("z", k)), times(dz, a0[k]))
-                    if a1[k] is not None:
-                        part["x", k] = add(part.get(("x", k)), a1[k])
+                    both = terms[0] if reach == 0 else terms[0] + terms[1]
+                    a0 = add(a0, both)
+                    if reach:
+                        a1 = add(a1, times(reach, terms[0] - terms[1]))
+                        if k is FIRST:
+                            a2 = add(a2, times(reach * reach, both))
+                if dy != 0:
+                    part["y"] = add(part.get("y"), a0)
                 if dz != 0:
-                    part["zz"] = add(part.get("zz"), times(dz * dz, a0[0]))
-                    if a1[0] is not None:
-                        part["xz"] = add(part.get("xz"), times(dz, a1[0]))
+                    part["z"] = add(part.get("z"), times(dz, a0))
+                    if k is FIRST:
+                        part["zz"] = add(part.get("zz"), times(dz * dz, a0))
+                        if a1 is not None:
+                            part["xz"] = add(part.get("xz"), times(dz, a1))
+                if a1 is not None:
+                    part["x"] = add(part.get("x"), a1)
                 if a2 is not None:
                     part["xx"] = add(part.get("xx"), a2)
-            for k in range(4):
-                if dy != 0:
-                    total["y", k] = add(total.get(("y", k)), times(dy, part["y", k]))
-                for name in ("x", "z"):
-                    if (name, k) in part:
-                        total[name, k] = add(total.get((name, k)), part[name, k])
-            if dy != 0:
-                total["yy"] = add(total.get("yy"), times(dy * dy, part["y", 0]))
-                for name, to in (("x", "xy"), ("z", "yz")):
-                    if (name, 0) in part:
-                        total[to] = add(total.get(to), times(dy, part[name, 0]))
-            for name in ("xx", "zz", "xz"):
+            for name in ("x", "z", "xx", "zz", "xz"):
                 if name in part:
                     total[name] = add(total.get(name), part[name])
-        for n, name in enumerate(ORDER):
-            sums[n, pl.ds(base, 2)] = total[name]
-        return carry
-
-    lax.fori_loop(0, 2, first_sums, 0)
-
-    for copy in copies[:2] + copies[4:]:
-        copy.wait_recv()
+            if dy != 0:
+                total["y"] = add(total.get("y"), times(dy, part["y"]))
+                if k is FIRST:
+                    total["yy"] = add(total.get("yy"), times(dy * dy, part["y"]))
+                    for name, to in (("x", "xy"), ("z", "yz")):
+                        if name in part:
+                            total[to] = add(total.get(to), times(dy, part[name]))
+        for n, name in enumerate(("x", "y", "z")):
+            if name in total:
+                at = 6 + 3 * k + n
+                sums[at] = total[name] if fresh or name == "y" else sums[at] + total[name]
+        for n, name in enumerate(ORDER[:6]):
+            if name in total:
+                sums[n] = total[name] if fresh or "y" in name else sums[n] + total[name]
+
+    def first_sums(dys, fresh):
+        gather_sums(FIRST, dys, fresh)
+
+        def feature(k, carry):
+            gather_sums(k, dys, fresh)
+            return carry
+
+        lax.fori_loop(1, 4, feature, 0)
+
+    see(0, flags)
+    hold_health((0,))
+    for f in range(5):
+        for t in range(4):
+            fields[3, f, t] = own[f][t]
+    first_sums((0,), True)
+
+    arrive(copies[2:4])
+    see(1, yrecv[0, 5])
+    see(-1, yrecv[1, 5])
+    hold_health(OTHERS)
+
+    side_lane = lane < 64
+    for f in range(5):
+        for t in range(4):
+            outer = jnp.where(side_lane, take(yrecv[0, f], to_x[t]), take(yrecv[1, f], to_x[t]))
+            for k in (1, 2, 3):
+                fields[3 + k, f, t] = jnp.where(y_at < k, outer, own[f][t])
+                fields[3 - k, f, t] = jnp.where(y_at >= 16 - k, outer, own[f][t])
+    first_sums(OTHERS, False)
+
+    arrive(copies[:2] + copies[4:])
     edge = [
         jnp.concatenate([xrecv[0, 4 * k : 4 * k + 4, :], xrecv[1, 4 * k : 4 * k + 4, :]], axis=0)
         for k in (4, 3, 0, 1, 2)
@@ -519,66 +575,53 @@
             for m, r in enumerate((0, 7)):
                 csend2[2 * m + k, n : n + 1, :] = tile[r : r + 1]
         for t in range(4):
-            xstress[n, t] = of_x[t]
+            ystress[3, n, t] = of_x[t]
 
     copies2 = exchange((xsend2, xrecv2), (ysend2, yrecv2), (csend2, crecv2), ssem2, rsem2)
 
     for n in range(9):
         for b in range(BYN):
             dg_out[pl.ds(4 * n + b, 8, stride=36), :] = block_tile([deform[t][n] for t in range(4)], b)
-    for copy in copies2[2:4]:
-        copy.wait_recv()
-
+    def second_sums(dys):
+        def component(c, carry):
+            total = force[c]
+            for dy in dys:
+                for dz in dz_of(dy):
+                    deep = COLUMNS[(dy, dz)]
+                    turn = -(8 * dy + dz)
+                    fixed = None
+                    if dy != 0:
+                        fixed = add(fixed, times(dy, ystress[dy + 3, 3 * c + 1]))
+                    if dz != 0:
+                        fixed = add(fixed, times(dz, ystress[dy + 3, 3 * c + 2]))
+                    if fixed is not None:
+                        fixed = spread(lane_roll(fixed, turn), deep)
+                    slope = spread(lane_roll(ystress[dy + 3, 3 * c], turn), deep) if deep else None
+                    for dx in range(-deep, deep + 1):
+                        lo = deep + dx
+                        value = None if fixed is None else fixed[lo : lo + 4]
+                        if dx != 0:
+                            value = add(value, times(dx, slope[lo : lo + 4]))
+                        if value is not None:
+                            total = total + weights[W_AT[(dy, dz)] + lo] * value
+            force[c] = total
+            return carry
+
+        lax.fori_loop(0, 3, component, 0)
+
+    second_sums((0,))
+    arrive(copies2[2:4])
     for n in range(9):
-        mine = [xstress[n, t] for t in range(4)]
-        beside = []
         for t in range(4):
-            beside.append(jnp.where(
-                side_lane, lane_roll(yrecv2[0, n], -32 * t), lane_roll(yrecv2[1, n], 32 * (3 - t))))
-
-        for s in range(-3, 7):
-            inner = extend(mine, row, s)
-            ystress[3, n, s + 3] = inner
-            if s < -2 or s > 5:
-                continue
-            outer = extend(beside, row, s)
+            inner = ystress[3, n, t]
+            outer = jnp.where(
+                side_lane, lane_roll(yrecv2[0, n], -32 * t), lane_roll(yrecv2[1, n], 32 * (3 - t)))
             for k in (1, 2, 3):
-                if k == 3 and not 0 <= s <= 3:
-                    continue
-                ystress[3 + k, n, s + 3] = jnp.where(y_at < k, outer, inner)
-                ystress[3 - k, n, s + 3] = jnp.where(y_at >= 16 - k, outer, inner)
-
-    def second_sums(c, carry):
-        total = force[c]
-        for dy in range(-3, 4):
-            for dz in range(-3, 4):
-                if (dy, dz) not in COLUMNS:
-                    continue
-                deep = COLUMNS[(dy, dz)]
-                turn = -(8 * dy + dz)
-                tiles = pl.ds(3 - deep, 4 + 2 * deep)
-                fixed = None
-                if dy != 0:
-                    fixed = add(fixed, times(dy, ystress[dy + 3, 3 * c + 1, tiles]))
-                if dz != 0:
-                    fixed = add(fixed, times(dz, ystress[dy + 3, 3 * c + 2, tiles]))
-                if fixed is not None:
-                    fixed = lane_roll(fixed, turn)
-                slope = lane_roll(ystress[dy + 3, 3 * c, tiles], turn) if deep else None
-                for dx in range(-deep, deep + 1):
-                    lo = deep + dx
-                    value = None if fixed is None else fixed[lo : lo + 4]
-                    if dx != 0:
-                        value = add(value, times(dx, slope[lo : lo + 4]))
-                    if value is not None:
-                        total = total + weights[W_AT[(dy, dz)] + lo] * value
-        force[c] = total
-        return carry
-
-    lax.fori_loop(0, 3, second_sums, 0)
-
-    for copy in copies2[:2] + copies2[4:]:
-        copy.wait_recv()
+                ystress[3 + k, n, t] = jnp.where(y_at < k, outer, inner)
+                ystress[3 - k, n, t] = jnp.where(y_at >= 16 - k, outer, inner)
+    second_sums(OTHERS)
+
+    arrive(copies2[:2] + copies2[4:])
 
     def corner2(low, high):
         return [
@@ -621,8 +664,11 @@
         full_force = [with_ends(force[c, t], end_force[c], row, t) for t in range(4)]
         for b in range(BYN):
             force_out[pl.ds(4 * c + b, 8, stride=12), :] = block_tile(full_force, b)
-    for copy in copies + copies2:
-        copy.wait_send()
+    for copy, tx, ty in copies + copies2:
+
+        @pl.when(present(tx, ty))
+        def _():
+            copy.wait_send()
 
 
 def store(dg, force, dg_out, force_out, sem):
@@ -664,17 +710,16 @@
             pltpu.VMEM((4, 8, LANES), f32),
             pltpu.VMEM((2, 9, 8, LANES), f32),
             pltpu.VMEM((2, 9, 8, LANES), f32),
-            pltpu.VMEM((2, 32, LANES), f32),
-            pltpu.VMEM((2, 32, LANES), f32),
-            pltpu.VMEM((4, 16, LANES), f32),
-            pltpu.VMEM((4, 16, LANES), f32),
-            pltpu.VMEM((7, 5, 10, 8, LANES), f32),
+            pltpu.VMEM((2, 27, LANES), f32),
+            pltpu.VMEM((2, 27, LANES), f32),
+            pltpu.VMEM((4, 9, LANES), f32),
+            pltpu.VMEM((4, 9, LANES), f32),
+            pltpu.VMEM((7, 5, 4, 8, LANES), f32),
             pltpu.VMEM((4, 4, 8, LANES), f32),
             pltpu.VMEM((7, 7, 4, 8, LANES), f32),
             pltpu.VMEM((W_COUNT, 4, 8, LANES), f32),
             pltpu.VMEM((18, 4, 8, LANES), f32),
-            pltpu.VMEM((7, 9, 10, 8, LANES), f32),
-            pltpu.VMEM((9, 4, 8, LANES), f32),
+            pltpu.VMEM((7, 9, 4, 8, LANES), f32),
             pltpu.VMEM((3, 4, 8, LANES), f32),
             pltpu.VMEM((len(ENDS) + 1, 8, LANES), f32),
             pltpu.SemaphoreType.DMA((5,)),

time: 31.2 us -> 28 us (0.90)
  the two profiles are of different devices: /device:TPU:25 before, /device:TPU:31 now
where the time goes in v4:
time: 28 us; the launch traced here: 27.8 us
  Pallas kernels  27.2 us (97%)
  between operations  0.64 us (2%)
    pallas_call x1, Pallas kernels, local(): pl.pallas_call(kernel, out_shape=(pltpu.VMEM((BXN * 9 * BYN, LANES), f32)...  26.5 us
    pallas_call x1, Pallas kernels, local(): pl.pallas_call(store, out_shape=(jax.ShapeDtypeStruct(dg.shape, f32), jax...  0.69 us

profile of v4, /device:TPU:31, one launch (start us, length us, event | category | flops | bytes accessed | tf_op | source)
XLA Modules:
  0.0 27.8 jit_solution(6611513046540175304)
XLA Ops:
  0.6 26.5 %peridynamics.1 = (f32[288,128]{1,0:T(8,128)S(1)}, f32[96,128]{1,0:T(8,128)S(1)}) custom-call(f32[96,128]{1,0:T(8,128)} %bitcast.15, f32[32,128]{1,0:T(8,128)} %bitcast.16, f32[32,128]{1,0:T(8,128)} %bitcast.17, s32[32,128]{1,0:T(8,128)} %bitcast.18, s32[4,162]{1,0:T(4,128)} %bitcast.19), custom_call_target="tpu_custom_call" | custom-call | tf_op jit(solution)/shard_map/peridynamics/pallas_call | solution.py:691
  27.1 0.7 %store.1 = (f32[288,128]{1,0:T(8,128)}, f32[96,128]{1,0:T(8,128)}) custom-call(f32[288,128]{1,0:T(8,128)S(1)} %get-tuple-element.6.dg, f32[96,128]{1,0:T(8,128)S(1)} %get-tuple-element.7.force), custom_call_target="tpu_custom_call" | custom-call | tf_op jit(solution)/shard_map/store/pallas_call | solution.py:736

commit v5 on v4

--- a/solution.py
+++ b/solution.py
@@ -20,6 +20,7 @@
     W_AT[_key] = _n
     _n += 2 * _m + 1
 W_COUNT = _n
+PLANE = 12
 CORNERS = ((-1, 1), (-1, -1), (1, 1), (1, -1))
 
 
@@ -117,9 +118,9 @@
 def kernel(
     disp_in, vol_in, hea_in, dam_in, pairs_in, dg_out, force_out,
     disp, vol, hea, dam, pairs,
-    ysend, yrecv, xsend, xrecv, csend, crecv,
+    ysend, yrecv, xsend, xrecv, csend, crecv, cpass,
     ysend2, yrecv2, xsend2, xrecv2, csend2, crecv2,
-    fields, own_u, health_m, weights, sums, ystress, force, end_weights,
+    fields, own_u, health_m, weights, sums, ystress, force, deform, end_weights,
     isem, ssem, rsem, ssem2, rsem2,
 ):
     loads = [
@@ -142,18 +143,30 @@
             return jnp.logical_and(inside[cx][0], inside[cy][1])
         return inside[cx][0] if cx else inside[cy][1]
 
+    early = jnp.logical_and(lax.rem(me_x, PLANE) == 0, inside[-1][0])
+    late = jnp.logical_and(lax.rem(me_x, PLANE) == PLANE - 1, inside[1][0])
+
+    def direct_to(cx, cy):
+        here = present(cx, cy)
+        return jnp.logical_and(here, jnp.logical_not(early)) if cx == -1 and cy else here
+
+    def direct_from(cx, cy):
+        here = present(cx, cy)
+        return jnp.logical_and(here, jnp.logical_not(late)) if cx == 1 and cy else here
+
     barrier = pltpu.get_barrier_semaphore()
+    waits = 0
     for cx in (-1, 0, 1):
         for cy in (-1, 0, 1):
             if cx or cy:
 
-                @pl.when(present(cx, cy))
+                @pl.when(direct_from(cx, cy))
                 def _():
                     pl.semaphore_signal(
                         barrier, inc=1, device_id=device(cx, cy), device_id_type=MESH)
 
-    spans = [
-        1 + inside[-1][axis].astype(jnp.int32) + inside[1][axis].astype(jnp.int32) for axis in (0, 1)]
+                waits = waits + direct_to(cx, cy).astype(jnp.int32)
+
     for n, cx in enumerate((-1, 1)):
 
         @pl.when(jnp.logical_not(present(cx, 0)))
@@ -172,12 +185,20 @@
 
         @pl.when(jnp.logical_not(present(cx, cy)))
         def _():
-            crecv[n] = jnp.zeros(crecv.shape[1:], jnp.float32)
             crecv2[n] = jnp.zeros(crecv2.shape[1:], jnp.float32)
 
     row, lane = iota(0), iota(1)
     block_y, y_in, z_at = lane // 32, (lane // 8) % 4, lane % 8
     y_at = lane // 8
+
+    for n, (cx, cy) in enumerate(CORNERS):
+        empty = jnp.logical_not(present(cx, cy))
+        if cx == 1:
+            empty = jnp.logical_and(empty, jnp.logical_not(late))
+
+        @pl.when(empty)
+        def _():
+            crecv[n] = jnp.zeros(crecv.shape[1:], jnp.float32)
 
     for load in loads:
         load.wait()
@@ -216,39 +237,57 @@
         xsend[m, 12:16, :] = vol[4 * r : 4 * r + 4, :]
         xsend[m, 16:20, :] = hea[4 * r : 4 * r + 4, :]
         xsend[m, 20:21, :] = flags[r : r + 1]
-    pl.semaphore_wait(barrier, spans[0] * spans[1] - 1)
-
-    def exchange(x_pair, y_pair, c_pair, sends, recvs):
-        moves = []
-        for n, cx in enumerate((-1, 1)):
-            moves.append((x_pair[0].at[1 - n], x_pair[1].at[n], -cx, 0))
-        for n, cy in enumerate((1, -1)):
-            moves.append((y_pair[0].at[n], y_pair[1].at[n], 0, -cy))
-        for n, (cx, cy) in enumerate(CORNERS):
-            at = 2 * (0 if cx == 1 else 1) + (0 if cy == 1 else 1)
-            moves.append((c_pair[0].at[at], c_pair[1].at[n], -cx, -cy))
+    pl.semaphore_wait(barrier, waits)
+
+    def y_moves(src, dst):
+        return [(src.at[n], dst.at[n], 0, -cy) for n, cy in enumerate((1, -1))]
+
+    def x_moves(src, dst):
+        return [(src.at[1 - n], dst.at[n], -cx, 0) for n, cx in enumerate((-1, 1))]
+
+    def corner_moves(src, dst):
+        return [
+            (src.at[2 * (0 if cx == 1 else 1) + (0 if cy == 1 else 1)], dst.at[n], -cx, -cy)
+            for n, (cx, cy) in enumerate(CORNERS)
+        ]
+
+    def exchange(moves, sends, recvs, first=0, to=present):
         copies = [
             (pltpu.make_async_remote_copy(
-                src_ref=src, dst_ref=dst, send_sem=sends.at[n], recv_sem=recvs.at[n],
+                src_ref=src, dst_ref=dst, send_sem=sends.at[first + n], recv_sem=recvs.at[first + n],
                 device_id=device(tx, ty), device_id_type=MESH), tx, ty)
             for n, (src, dst, tx, ty) in enumerate(moves)
         ]
         for copy, tx, ty in copies:
 
-            @pl.when(present(tx, ty))
+            @pl.when(to(tx, ty))
             def _():
                 copy.start()
 
         return copies
 
-    def arrive(copies):
+    def arrive(copies, come=present):
         for copy, tx, ty in copies:
 
-            @pl.when(present(-tx, -ty))
+            @pl.when(come(-tx, -ty))
             def _():
                 copy.wait_recv()
 
-    copies = exchange((xsend, xrecv), (ysend, yrecv), (csend, crecv), ssem, rsem)
+    copies = exchange(
+        corner_moves(csend, crecv) + x_moves(xsend, xrecv) + y_moves(ysend, yrecv),
+        ssem, rsem, to=direct_to)
+
+    around = pltpu.make_async_remote_copy(
+        src_ref=cpass, dst_ref=crecv.at[2:4], send_sem=ssem.at[8], recv_sem=rsem.at[8],
+        device_id=device(-1, 0), device_id_type=MESH)
+
+    @pl.when(early)
+    def _():
+        arrive(copies[6:])
+        for n in range(2):
+            for f in range(6):
+                cpass[n, f : f + 1, :] = yrecv[n, f, 0:1, :]
+        around.start()
 
     to_x = [16 * z_at + 4 * y_in + t for t in range(4)]
 
@@ -392,7 +431,7 @@
             fields[3, f, t] = own[f][t]
     first_sums((0,), True)
 
-    arrive(copies[2:4])
+    arrive(copies[6:], lambda cx, cy: jnp.logical_and(present(cx, cy), jnp.logical_not(early)))
     see(1, yrecv[0, 5])
     see(-1, yrecv[1, 5])
     hold_health(OTHERS)
@@ -406,7 +445,27 @@
                 fields[3 - k, f, t] = jnp.where(y_at >= 16 - k, outer, own[f][t])
     first_sums(OTHERS, False)
 
-    arrive(copies[:2] + copies[4:])
+    def end_pack(tile_of):
+        got = jnp.zeros((8, LANES), jnp.float32)
+        for t in range(3):
+            got = jnp.where(row == t, tile_of(t)[0:1], got)
+            got = jnp.where(row == 6 - t, tile_of(t + 1)[7:8], got)
+        return got
+
+    end_sums = [end_pack(lambda t: sums[n, t]) for n in range(18)]
+    end_u = [end_pack(lambda t: own_u[c, t]) for c in range(4)]
+    end_volume = end_pack(lambda t: own[1][t])
+
+    def row_sum(tile):
+        tile = tile + jnp.where(row % 2 == 0, row_roll(tile, -1), row_roll(tile, 1))
+        return tile + jnp.where(row % 4 < 2, row_roll(tile, -2), row_roll(tile, 2))
+
+    arrive(copies[:6], direct_from)
+
+    @pl.when(late)
+    def _():
+        around.wait_recv()
+
     edge = [
         jnp.concatenate([xrecv[0, 4 * k : 4 * k + 4, :], xrecv[1, 4 * k : 4 * k + 4, :]], axis=0)
         for k in (4, 3, 0, 1, 2)
@@ -414,9 +473,7 @@
     edge = edge[:2] + [edge[1] * e for e in edge[2:]]
 
     def edge_tile(f, t):
-        got = jnp.where(row % 4 == block_y, take(edge[f], to_x[t]), 0.0)
-        got = got + jnp.where(row % 2 == 0, row_roll(got, -1), row_roll(got, 1))
-        return got + jnp.where(row % 4 < 2, row_roll(got, -2), row_roll(got, 2))
+        return row_sum(jnp.where(row % 4 == block_y, take(edge[f], to_x[t]), 0.0))
 
     corner_low = [
         jnp.where(side_lane, take(crecv[0], to_x[t]), take(crecv[1], to_x[t])) for t in range(4)]
@@ -520,25 +577,14 @@
     end_weights[len(ENDS)] = w
     three = {("x", k): step_three * (w * end_fields[3][k + 1]) for k in range(4)}
     three["xx"] = step_three * three["x", 0]
-    end_sums = [ends_of(row, end_total[name], three.get(name, 0.0)) for name in ORDER]
-
-    to_raw = [8 * (4 * b + (lane // 4) % 4) + lane // 16 for b in range(BYN)]
-    x_in = lane % 4
-
-    def block_tile(of_x, b):
-        got = take(of_x[0], to_raw[b])
-        for t in range(1, 4):
-            got = jnp.where(x_in == t, take(of_x[t], to_raw[b]), got)
-        return got
-
-    deform, stress = [], []
-    for t in range(4):
-        full = [with_ends(sums[n, t], end_sums[n], row, t) for n in range(18)]
+    end_more = [ends_of(row, end_total[name], three.get(name, 0.0)) for name in ORDER]
+
+    def material(full, u):
         kxx, kxy, kxz, kyy, kyz, kzz = full[:6]
         span = full[6:9]
         sym = [kxx, kxy, kxz, kxy, kyy, kyz, kxz, kyz, kzz]
         moment = [
-            sym[3 * c + d] + full[9 + 3 * c + d] - own_u[c, t] * span[d]
+            sym[3 * c + d] + full[9 + 3 * c + d] - u[c] * span[d]
             for c in range(3) for d in range(3)
         ]
         shape = [sym[n] + 1.0 if n % 4 == 0 else sym[n] for n in range(9)]
@@ -552,19 +598,45 @@
             trace + 2.0 * SHEAR * strain[n] if n % 4 == 0 else 2.0 * SHEAR * strain[n]
             for n in range(9)
         ]
-        first = [e * own_u[3, t] for e in product(grad, second)]
-        mapped = product(first, inv)
+        first = [e * u[3] for e in product(grad, second)]
+        return grad, product(first, inv)
+
+    _, end_mapped = material([a + b for a, b in zip(end_sums, end_more)], end_u)
+    for n in range(9):
+        tile = end_volume * end_mapped[n]
+        xsend2[0, 3 * n : 3 * n + 3, :] = tile[0:3]
+        xsend2[1, 3 * n : 3 * n + 3, :] = tile[4:7]
+        for k, slot in enumerate((0, 3)):
+            wide_tile = take(tile, 32 * slot + lane % 32)
+            wide_tile = jnp.where(block_y == row % 4, wide_tile, 0.0)
+            wide_tile = wide_tile + (row_roll(wide_tile, -1) + row_roll(wide_tile, -2))
+            for m in range(2):
+                csend2[2 * m + k, n : n + 1, :] = wide_tile[4 * m : 4 * m + 1]
+    copies2 = exchange(corner_moves(csend2, crecv2) + x_moves(xsend2, xrecv2), ssem2, rsem2)
+
+    to_raw = [8 * (4 * b + (lane // 4) % 4) + lane // 16 for b in range(BYN)]
+    x_in = lane % 4
+
+    def block_tile(of_x, b):
+        got = take(of_x[0], to_raw[b])
+        for t in range(1, 4):
+            got = jnp.where(x_in == t, take(of_x[t], to_raw[b]), got)
+        return got
+
+    stress = []
+    for t in range(4):
+        full = [with_ends(sums[n, t], end_more[n], row, t) for n in range(18)]
+        grad, mapped = material(full, [own_u[c, t] for c in range(4)])
+        span = full[6:9]
         for c in range(3):
             force[c, t] = mapped[3 * c] * span[0] + mapped[3 * c + 1] * span[1] + mapped[3 * c + 2] * span[2]
         v = own[1][t]
-        deform.append(grad)
+        for n in range(9):
+            deform[n, t] = grad[n]
         stress.append([v * e for e in mapped])
 
     for n in range(9):
         of_x = [stress[t][n] for t in range(4)]
-        for t in range(3):
-            xsend2[0, 3 * n + t : 3 * n + t + 1, :] = of_x[t][0:1]
-            xsend2[1, 3 * n + t : 3 * n + t + 1, :] = of_x[t + 1][7:8]
         low = of_x[0]
         high = lane_roll(of_x[0], 32)
         for t in range(1, 4):
@@ -572,16 +644,11 @@
             high = jnp.where(block_y == t, lane_roll(of_x[t], 32 * (t - 3)), high)
         for k, tile in enumerate((low, high)):
             ysend2[k, n] = tile
-            for m, r in enumerate((0, 7)):
-                csend2[2 * m + k, n : n + 1, :] = tile[r : r + 1]
         for t in range(4):
             ystress[3, n, t] = of_x[t]
 
-    copies2 = exchange((xsend2, xrecv2), (ysend2, yrecv2), (csend2, crecv2), ssem2, rsem2)
-
-    for n in range(9):
-        for b in range(BYN):
-            dg_out[pl.ds(4 * n + b, 8, stride=36), :] = block_tile([deform[t][n] for t in range(4)], b)
+    copies2 += exchange(y_moves(ysend2, yrecv2), ssem2, rsem2, 6)
+
     def second_sums(dys):
         def component(c, carry):
             total = force[c]
@@ -610,7 +677,11 @@
         lax.fori_loop(0, 3, component, 0)
 
     second_sums((0,))
-    arrive(copies2[2:4])
+    for n in range(9):
+        for b in range(BYN):
+            dg_out[pl.ds(4 * n + b, 8, stride=36), :] = block_tile([deform[n, t] for t in range(4)], b)
+
+    arrive(copies2[6:])
     for n in range(9):
         for t in range(4):
             inner = ystress[3, n, t]
@@ -621,18 +692,23 @@
                 ystress[3 - k, n, t] = jnp.where(y_at >= 16 - k, outer, inner)
     second_sums(OTHERS)
 
-    arrive(copies2[:2] + copies2[4:])
-
-    def corner2(low, high):
+    for c in range(3):
+        for b in range(BYN):
+            force_out[pl.ds(4 * c + b, 8, stride=12), :] = block_tile([force[c, t] for t in range(4)], b)
+
+    arrive(copies2[:6])
+
+    def corner2(low, high, slots):
         return [
-            jnp.where(lane[0:1] < 64, lane_roll(crecv2[low], -32 * t), lane_roll(crecv2[high], 32 * (3 - t)))
-            for t in range(4)
+            jnp.where(lane[0:1] < 64, lane_roll(crecv2[low], -32 * k), lane_roll(crecv2[high], 32 * (3 - k)))
+            for k in slots
         ]
 
-    corner_low2, corner_high2 = corner2(0, 1), corner2(2, 3)
+    corner_low2, corner_high2 = corner2(0, 1, (3, 2, 1, 0)), corner2(2, 3, (0, 1, 2, 3))
 
     def halo_row(n, low, t):
-        return xrecv2[0, 3 * n + t - 1 : 3 * n + t, :] if low else xrecv2[1, 3 * n + t : 3 * n + t + 1, :]
+        at = 3 * n + (3 - t if low else t)
+        return xrecv2[0 if low else 1, at : at + 1, :]
 
     end_inner, end_outer, end_force = [], [], []
     for n in range(9):
@@ -660,15 +736,22 @@
                 total = add(total, end_weights[ENDS.index((dy, dz))] * value)
         three = step_three * place(row, REACH_THREE, lambda low, t: halo_row(3 * c, low, t))
         end_force.append(ends_of(row, total, end_weights[len(ENDS)] * three))
+    own_x = jnp.where(low_end, row, 7 - row)
     for c in range(3):
-        full_force = [with_ends(force[c, t], end_force[c], row, t) for t in range(4)]
         for b in range(BYN):
-            force_out[pl.ds(4 * c + b, 8, stride=12), :] = block_tile(full_force, b)
-    for copy, tx, ty in copies + copies2:
-
-        @pl.when(present(tx, ty))
-        def _():
-            copy.wait_send()
+            at = pl.ds(4 * c + b, 8, stride=12)
+            more = row_sum(jnp.where(x_in == own_x, take(end_force[c], to_raw[b]), 0.0))
+            force_out[at, :] = force_out[at, :] + jnp.where(row % 7 == 0, more, 0.0)
+    for group, to in ((copies, direct_to), (copies2, present)):
+        for copy, tx, ty in group:
+
+            @pl.when(to(tx, ty))
+            def _():
+                copy.wait_send()
+
+    @pl.when(early)
+    def _():
+        around.wait_send()
 
 
 def store(dg, force, dg_out, force_out, sem):
@@ -708,6 +791,7 @@
             pltpu.VMEM((2, 24, LANES), f32),
             pltpu.VMEM((4, 8, LANES), f32),
             pltpu.VMEM((4, 8, LANES), f32),
+            pltpu.VMEM((2, 8, LANES), f32),
             pltpu.VMEM((2, 9, 8, LANES), f32),
             pltpu.VMEM((2, 9, 8, LANES), f32),
             pltpu.VMEM((2, 27, LANES), f32),
@@ -721,10 +805,11 @@
             pltpu.VMEM((18, 4, 8, LANES), f32),
             pltpu.VMEM((7, 9, 4, 8, LANES), f32),
             pltpu.VMEM((3, 4, 8, LANES), f32),
+            pltpu.VMEM((9, 4, 8, LANES), f32),
             pltpu.VMEM((len(ENDS) + 1, 8, LANES), f32),
             pltpu.SemaphoreType.DMA((5,)),
-            pltpu.SemaphoreType.DMA((8,)),
-            pltpu.SemaphoreType.DMA((8,)),
+            pltpu.SemaphoreType.DMA((9,)),
+            pltpu.SemaphoreType.DMA((9,)),
             pltpu.SemaphoreType.DMA((8,)),
             pltpu.SemaphoreType.DMA((8,)),
         ],

time: 28 us -> 27.1 us (0.968)
  Pallas kernels: 27.2 us -> 26.3 us
    pallas_call x1, Pallas kernels: 26.5 us -> 25.6 us  [local(): pl.pallas_call(kernel, out_shape=(pltpu.VMEM((BXN * 9 * BYN, LANES), f32)...]
where the time goes in v5:
time: 27.1 us; the launch traced here: 26.9 us
  Pallas kernels  26.3 us (97%)
  between operations  0.64 us (2%)
    pallas_call x1, Pallas kernels, local(): pl.pallas_call(kernel, out_shape=(pltpu.VMEM((BXN * 9 * BYN, LANES), f32)...  25.6 us
    pallas_call x1, Pallas kernels, local(): pl.pallas_call(store, out_shape=(jax.ShapeDtypeStruct(dg.shape, f32), jax...  0.69 us

profile of v5, /device:TPU:31, one launch (start us, length us, event | category | flops | bytes accessed | tf_op | source)
XLA Modules:
  0.0 26.9 jit_solution(13299582079392569205)
XLA Ops:
  0.6 25.6 %peridynamics.1 = (f32[288,128]{1,0:T(8,128)S(1)}, f32[96,128]{1,0:T(8,128)S(1)}) custom-call(f32[96,128]{1,0:T(8,128)} %bitcast.15, f32[32,128]{1,0:T(8,128)} %bitcast.16, f32[32,128]{1,0:T(8,128)} %bitcast.17, s32[32,128]{1,0:T(8,128)} %bitcast.18, s32[4,162]{1,0:T(4,128)} %bitcast.19), custom_call_target="tpu_custom_call" | custom-call | tf_op jit(solution)/shard_map/peridynamics/pallas_call | solution.py:774
  26.3 0.7 %store.1 = (f32[288,128]{1,0:T(8,128)}, f32[96,128]{1,0:T(8,128)}) custom-call(f32[288,128]{1,0:T(8,128)S(1)} %get-tuple-element.6.dg, f32[96,128]{1,0:T(8,128)S(1)} %get-tuple-element.7.force), custom_call_target="tpu_custom_call" | custom-call | tf_op jit(solution)/shard_map/store/pallas_call | solution.py:821

commit v6 on v5

--- a/solution.py
+++ b/solution.py
@@ -121,7 +121,7 @@
     ysend, yrecv, xsend, xrecv, csend, crecv, cpass,
     ysend2, yrecv2, xsend2, xrecv2, csend2, crecv2,
     fields, own_u, health_m, weights, sums, ystress, force, deform, end_weights,
-    isem, ssem, rsem, ssem2, rsem2,
+    isem, ssem, rsem, ssem2, rsem2, ready,
 ):
     loads = [
         pltpu.make_async_copy(src, dst, isem.at[n])
@@ -148,7 +148,7 @@
 
     def direct_to(cx, cy):
         here = present(cx, cy)
-        return jnp.logical_and(here, jnp.logical_not(early)) if cx == -1 and cy else here
+        return jnp.logical_and(here, jnp.logical_not(early)) if cx == -1 else here
 
     def direct_from(cx, cy):
         here = present(cx, cy)
@@ -160,7 +160,11 @@
         for cy in (-1, 0, 1):
             if cx or cy:
 
-                @pl.when(direct_from(cx, cy))
+                greet = present(cx, cy)
+                if cx == 1:
+                    greet = jnp.logical_and(greet, jnp.logical_not(late))
+
+                @pl.when(greet)
                 def _():
                     pl.semaphore_signal(
                         barrier, inc=1, device_id=device(cx, cy), device_id_type=MESH)
@@ -239,6 +243,10 @@
         xsend[m, 20:21, :] = flags[r : r + 1]
     pl.semaphore_wait(barrier, waits)
 
+    @pl.when(late)
+    def _():
+        pl.semaphore_signal(ready, inc=1, device_id=device(1, 0), device_id_type=MESH)
+
     def y_moves(src, dst):
         return [(src.at[n], dst.at[n], 0, -cy) for n, cy in enumerate((1, -1))]
 
@@ -280,14 +288,6 @@
     around = pltpu.make_async_remote_copy(
         src_ref=cpass, dst_ref=crecv.at[2:4], send_sem=ssem.at[8], recv_sem=rsem.at[8],
         device_id=device(-1, 0), device_id_type=MESH)
-
-    @pl.when(early)
-    def _():
-        arrive(copies[6:])
-        for n in range(2):
-            for f in range(6):
-                cpass[n, f : f + 1, :] = yrecv[n, f, 0:1, :]
-        around.start()
 
     to_x = [16 * z_at + 4 * y_in + t for t in range(4)]
 
@@ -431,7 +431,7 @@
             fields[3, f, t] = own[f][t]
     first_sums((0,), True)
 
-    arrive(copies[6:], lambda cx, cy: jnp.logical_and(present(cx, cy), jnp.logical_not(early)))
+    arrive(copies[6:])
     see(1, yrecv[0, 5])
     see(-1, yrecv[1, 5])
     hold_health(OTHERS)
@@ -444,6 +444,15 @@
                 fields[3 + k, f, t] = jnp.where(y_at < k, outer, own[f][t])
                 fields[3 - k, f, t] = jnp.where(y_at >= 16 - k, outer, own[f][t])
     first_sums(OTHERS, False)
+
+    @pl.when(early)
+    def _():
+        for n in range(2):
+            for f in range(6):
+                cpass[n, f : f + 1, :] = yrecv[n, f, 0:1, :]
+        pl.semaphore_wait(ready, 1)
+        copies[5][0].start()
+        around.start()
 
     def end_pack(tile_of):
         got = jnp.zeros((8, LANES), jnp.float32)
@@ -742,7 +751,7 @@
             at = pl.ds(4 * c + b, 8, stride=12)
             more = row_sum(jnp.where(x_in == own_x, take(end_force[c], to_raw[b]), 0.0))
             force_out[at, :] = force_out[at, :] + jnp.where(row % 7 == 0, more, 0.0)
-    for group, to in ((copies, direct_to), (copies2, present)):
+    for group, to in ((copies[:4], direct_to), (copies[4:] + copies2, present)):
         for copy, tx, ty in group:
 
             @pl.when(to(tx, ty))
@@ -812,6 +821,7 @@
             pltpu.SemaphoreType.DMA((9,)),
             pltpu.SemaphoreType.DMA((8,)),
             pltpu.SemaphoreType.DMA((8,)),
+            pltpu.SemaphoreType.REGULAR,
         ],
         compiler_params=pltpu.CompilerParams(collective_id=0, has_side_effects=True),
         name="peridynamics",

time: 27.1 us -> 27 us (level)
  no operation moved by 1% of the time
where the time goes in v6:
time: 27 us; the launch traced here: 26.8 us
  Pallas kernels  26.2 us (97%)
  between operations  0.64 us (2%)
    pallas_call x1, Pallas kernels, local(): pl.pallas_call(kernel, out_shape=(pltpu.VMEM((BXN * 9 * BYN, LANES), f32)...  25.5 us
    pallas_call x1, Pallas kernels, local(): pl.pallas_call(store, out_shape=(jax.ShapeDtypeStruct(dg.shape, f32), jax...  0.69 us

profile of v6, /device:TPU:31, one launch (start us, length us, event | category | flops | bytes accessed | tf_op | source)
XLA Modules:
  0.0 26.8 jit_solution(16721982910444402084)
XLA Ops:
  0.6 25.5 %peridynamics.1 = (f32[288,128]{1,0:T(8,128)S(1)}, f32[96,128]{1,0:T(8,128)S(1)}) custom-call(f32[96,128]{1,0:T(8,128)} %bitcast.15, f32[32,128]{1,0:T(8,128)} %bitcast.16, f32[32,128]{1,0:T(8,128)} %bitcast.17, s32[32,128]{1,0:T(8,128)} %bitcast.18, s32[4,162]{1,0:T(4,128)} %bitcast.19), custom_call_target="tpu_custom_call" | custom-call | tf_op jit(solution)/shard_map/peridynamics/pallas_call | solution.py:783
  26.1 0.7 %store.1 = (f32[288,128]{1,0:T(8,128)}, f32[96,128]{1,0:T(8,128)}) custom-call(f32[288,128]{1,0:T(8,128)S(1)} %get-tuple-element.6.dg, f32[96,128]{1,0:T(8,128)S(1)} %get-tuple-element.7.force), custom_call_target="tpu_custom_call" | custom-call | tf_op jit(solution)/shard_map/store/pallas_call | solution.py:831
